TPU v7x, 256 devices: a whole 4x4x8 slice. The times are simulated.
256 devices in a mesh: lon: 16 (over y_lo, x, core), lat: 16 (over z, y_hi).
Axes of the slice: x: 4, y: 4 (y_hi: 2, y_lo: 2; y = y_hi * 2 + y_lo), z: 8, core: 2. Of those that a mesh axis runs over, the one named last changes fastest.
Arguments:
- tracers: bfloat16 [12, 64, 128, 2048], P(None, None, 'lat', 'lon'), may hold values from 0.099609375 to 2
- east_wind: bfloat16 [64, 128, 2048], P(None, 'lat', 'lon'), may hold values from -0.44921875 to 0.44921875
- north_wind: bfloat16 [64, 128, 2048], P(None, 'lat', 'lon'), may hold values from -0.44921875 to 0.44921875
- sunlit: int32 [128, 2048], P('lat', 'lon'), may hold values from 0 to 1, as said below
- coupling: float32 [12, 12], replicated, may hold values from -0.15 to 0.15
- rate_table: float32 [8, 64], replicated, may hold values from 0.01 to 0.6
- rate_index: int32 [12], replicated, may hold values from 0 to 7
- kappa: float32 [63], replicated, may hold values from 0.05 to 0.24
Outputs:
- updated: bfloat16 [12, 64, 128, 2048], P(None, None, 'lat', 'lon')
Inputs may be any that keep to these rules, and one draw needn't show every extreme that they name: A device's block of columns holds at most 768 sunlit columns, and together with the block of the device half the lon axis away (same lat index) at most 1024; both bounds are reached in every draw.
All inputs are finite; a program needn't handle non-finite values.
Results may differ from a plain program's by a relative error of at most 0.001.
Values may be sent and summed in bfloat16 or wider, within the bound.
No kernel may reach another device: no remote copies, remote signals or barrier semaphores. Data moves between devices by JAX's collectives and lax.ppermute only.
A program may use at most 128 MiB of HBM per device.

v0:
```python
import jax
import jax.numpy as jnp
from jax import lax
from jax.sharding import PartitionSpec as P

SUBSTEPS = 16


def padded(cells, sides, width, closed):
    for axis, dim in sides:
        count = lax.axis_size(axis)
        ends = count if closed else count - 1
        head = lax.slice_in_dim(cells, 0, width, axis=dim)
        tail = lax.slice_in_dim(cells, cells.shape[dim] - width, cells.shape[dim], axis=dim)
        cells = jnp.concatenate(
            [
                lax.ppermute(tail, axis, [(i, (i + 1) % count) for i in range(ends)]),
                cells,
                lax.ppermute(head, axis, [((i + 1) % count, i) for i in range(ends)]),
            ],
            axis=dim,
        )
    return cells


def chemistry(start, coupling, loss, kappa):
    species, levels, columns = start.shape
    state = start.astype(jnp.float32)
    kappa_full = jnp.concatenate([kappa, jnp.zeros((1,), jnp.float32)])[None, :, None]

    def substep(step, state):
        made = jnp.dot(
            coupling, state.reshape(species, levels * columns), precision=lax.Precision.HIGHEST
        )
        state = (state + made.reshape(species, levels, columns)) / (
            1.0 + loss[:, :, None] * (1.0 + state * state)
        )
        flux = kappa_full * (jnp.roll(state, -1, axis=1) - state)
        return state + flux - jnp.roll(flux, 1, axis=1)

    return lax.fori_loop(0, SUBSTEPS, substep, state)


def face_flux(speed, behind, ahead):
    return jnp.maximum(speed, 0.0) * behind + jnp.minimum(speed, 0.0) * ahead


def advect(tracers, east_wind, north_wind):
    species = tracers.shape[0]
    lat_rows = tracers.shape[2]
    conc = tracers.astype(jnp.float32)
    speed_east = east_wind.astype(jnp.float32)[None]
    zonal_rims = jnp.concatenate([tracers[..., :1], tracers[..., -1:]], axis=3)
    east_rims = jnp.concatenate([east_wind[..., :1], east_wind[..., -1:]], axis=2)[None]
    zonal_edges = jnp.concatenate([zonal_rims, east_rims], axis=0)
    wide = padded(zonal_edges, (("lon", 3),), 1, True).astype(jnp.float32)
    west_cell = jnp.concatenate([wide[:species, :, :, 0:1], conc[..., :-1]], axis=3)
    west_flux = face_flux(speed_east, west_cell, conc)
    edge_east = face_flux(wide[species:, :, :, 3:4], conc[..., -1:], wide[:species, :, :, 3:4])
    east_flux = jnp.concatenate([west_flux[..., 1:], edge_east], axis=3)
    merid_rims = jnp.concatenate([tracers[:, :, :1], tracers[:, :, -1:]], axis=2)
    north_rims = jnp.concatenate([north_wind[:, :1], north_wind[:, -1:]], axis=1)[None]
    merid_edges = jnp.concatenate([merid_rims, north_rims], axis=0)
    tall = padded(merid_edges, (("lat", 2),), 1, False).astype(jnp.float32)
    global_row = lax.axis_index("lat") * lat_rows + jnp.arange(lat_rows, dtype=jnp.int32)
    speed_north = jnp.where((global_row == 0)[None, :, None], 0.0, north_wind.astype(jnp.float32))[
        None
    ]
    south_cell = jnp.concatenate([tall[:species, :, 0:1], conc[:, :, :-1]], axis=2)
    south_flux = face_flux(speed_north, south_cell, conc)
    edge_north = face_flux(tall[species:, :, 3:4], conc[:, :, -1:], tall[:species, :, 3:4])
    north_flux = jnp.concatenate([south_flux[:, :, 1:], edge_north], axis=2)
    return (conc - (east_flux - west_flux) - (north_flux - south_flux)).astype(jnp.bfloat16)


def local(tracers, east_wind, north_wind, sunlit, coupling, rate_table, rate_index, kappa):
    species, levels, lat_rows, lon_cols = tracers.shape
    columns = lat_rows * lon_cols
    advected = advect(tracers, east_wind, north_wind).reshape(species, levels, columns)
    light = sunlit.reshape(columns)
    rate_rows = rate_table.shape[0]
    picker = (rate_index[:, None] == jnp.arange(rate_rows, dtype=jnp.int32)[None, :]).astype(
        jnp.float32
    )
    loss = jnp.sum(picker[:, :, None] * rate_table[None, :, :], axis=1)
    finished = chemistry(advected, coupling, loss, kappa).astype(jnp.bfloat16)
    result = jnp.where(light[None, None, :] > 0, finished, advected)
    return result.reshape(species, levels, lat_rows, lon_cols)


def solution(mesh):
    placed = (
        P(None, None, "lat", "lon"),
        P(None, "lat", "lon"),
        P(None, "lat", "lon"),
        P("lat", "lon"),
        P(),
        P(),
        P(),
        P(),
    )
    return jax.shard_map(
        local, mesh=mesh, in_specs=placed, out_specs=P(None, None, "lat", "lon"), check_vma=False
    )
```

profile of v0, /device:TPU:113, one launch (start us, length us, event | category | flops | bytes accessed | tf_op | source)
XLA Modules:
  0.0 388.9 jit_solution(2663954439055585634)
XLA Ops:
  15.9 4.5 %collective-permute-start.2 = (bf16[13,64,1,128]{3,1,2,0:T(8,128)(2,1)}, bf16[13,64,1,128]{3,1,2,0:T(8,128)(2,1)}, u32[]{:S(2)}, u32[]{:S(2)}) collective-permute-start(bf16[13,64,1,128]{3,1,2,0:T(8,128)(2,1)} %copy.65), channel_id=1, source_target_pairs={{0,1},{1,2},{2,3},{3,4},{4,5},{5,6},{6,7},{7,8},{8,9},{9,10},{10,1... | collective-permute-start | bytes 638984 | tf_op jit(solution)/shard_map/ppermute | solution.py:17
  63.6 5.9 %maximum_convert_fusion = f32[12,64,1,128]{1,2,3,0:T(1,128)S(1)} fusion(bf16[13,64,1,128]{1,2,3,0:T(2,128)(2,1)} %copy.68, bf16[13,64,1,128]{1,2,3,0:T(2,128)(2,1)} %copy.67, bf16[1,64,2,128]{1,2,3,0:T(2,128)(2,1)S(1)} %maximum_bitcast_fusion, bf16[12,64,1,128]{1,2,3,0:T(2,128)(2,1)} %get-tuple-element.65, bf16[12,64,1,128]{1,2,3,0:T(2,128)(2,1)} %get-tuple-element.64), kind=kLoop, calls=%fused_computation.28 | loop fusion | flops 983040 | bytes 1245184 | tf_op jit(solution)/shard_map/slice | solution.py:69
  69.7 6.3 %fusion.10 = (f32[12,64,8,128]{1,2,3,0:T(8,128)S(1)}, f32[12,64,8,128]{1,2,3,0:T(8,128)S(1)}) fusion(f32[12,64,7,128]{1,2,3,0:T(8,128)} %slice.127, f32[12,64,1,128]{1,2,3,0:T(1,128)S(1)} %maximum_convert_fusion, bf16[12,64,8,128]{1,2,3,0:T(8,128)(2,1)S(1)} %copy.53, f32[64,8,128]{0,1,2:T(8,128)S(1)} %copy-done.7, f32[64,8,128]{0,1,2:T(8,128)S(1)} %copy-done.6, ...), kind=kLoop, calls=%fused_computation.15 | loop fusion | flops 7077888 | bytes 15204352 | tf_op jit(solution)/shard_map/add | solution.py:45
  82.4 7.5 %fusion.14 = f32[12,64,1,128]{1,2,3,0:T(1,128)S(1)} fusion(bf16[13,64,1,128]{1,2,3,0:T(2,128)(2,1)S(1)} %copy-done.5, bf16[13,64,1,128]{1,2,3,0:T(2,128)(2,1)S(1)} %copy-done.4, bf16[1,64,2,128]{1,2,3,0:T(2,128)(2,1)S(1)} %maximum_bitcast_fusion, bf16[12,64,1,128]{1,2,3,0:T(2,128)(2,1)S(1)} %copy-done.2, bf16[12,64,1,128]{1,2,3,0:T(2,128)(2,1)S(1)} %copy-done.1, ...), kind=kLoop, calls=%fused_computation.23 | loop fusion | flops 1277952 | bytes 1703936 | tf_op jit(solution)/shard_map/add | solution.py:45
  90.0 7.3 %fusion.9 = bf16[12,64,8,128]{1,2,3,0:T(8,128)(2,1)} fusion(f32[12,64,8,128]{1,2,3,0:T(8,128)S(1)} %get-tuple-element.63, f32[12,64,8,1]{1,2,3,0:T(8,128)S(1)} %fusion.17, f32[12,64,8,127]{1,2,3,0:T(8,128)} %slice.121, f32[12,64,8,128]{1,2,3,0:T(8,128)S(1)} %get-tuple-element.62, f32[12,64,1,128]{1,2,3,0:T(1,128)S(1)} %fusion.14, ...), kind=kLoop, calls=%fused_computation.13 | loop fusion | flops 6291456 | bytes 15728640 | tf_op jit(solution)/shard_map/convert_element_type | solution.py:73
  105.1 277.8 %while.10 = (s32[]{:T(128)}, f32[12,64,1024]{2,0,1:T(8,128)}, f32[12,12]{1,0:T(8,128)S(1)}, f32[12,64]{0,1:T(8,128)S(1)}, f32[1,64,1]{1,2,0:T(1,128)S(1)}, /*index=5*/s32[]{:T(128)}) while((s32[]{:T(128)}, f32[12,64,1024]{2,0,1:T(8,128)}, f32[12,12]{1,0:T(8,128)S(1)}, f32[12,64]{0,1:T(8,128)S(1)}, f32[1,64,1]{1,2,0:T(1,128)S(1)}, ...), condition=%wide.region_2.3_spmd, body=%wide.region_1.2_spmd.sunk | while | flops 122683392 | bytes 69210016 | solution.py:41
  105.1 4.0 %copy.91 = f32[12,64,1024]{2,1,0:T(8,128)S(1)} copy(f32[12,64,1024]{2,0,1:T(8,128)} %get-tuple-element.118) | data formatting | bytes 6291456 | tf_op jit(solution)/shard_map
  111.3 6.2 %add_divide_fusion.2 = f32[12,64,1024]{2,0,1:T(8,128)S(1)} fusion(f32[12,64,1024]{2,0,1:T(8,128)S(1)} %copy-done, f32[64,1024,12]{1,0,2:T(8,128)S(1)} %slice_bitcast_fusion.2, f32[12,64]{0,1:T(8,128)S(1)} %get-tuple-element.126, f32[12,12]{1,0:T(8,128)S(1)} %get-tuple-element.125), kind=kOutput, calls=%fused_computation.5.clone.1 | convolution fusion | flops 117964800 | bytes 9440832 | tf_op jit(solution)/shard_map/while/body/eval_jaxpr/dot_general | solution.py:32
  122.5 4.0 %copy.91 = f32[12,64,1024]{2,1,0:T(8,128)S(1)} copy(f32[12,64,1024]{2,0,1:T(8,128)} %get-tuple-element.118) | data formatting | bytes 6291456 | tf_op jit(solution)/shard_map
  128.7 6.2 %add_divide_fusion.2 = f32[12,64,1024]{2,0,1:T(8,128)S(1)} fusion(f32[12,64,1024]{2,0,1:T(8,128)S(1)} %copy-done, f32[64,1024,12]{1,0,2:T(8,128)S(1)} %slice_bitcast_fusion.2, f32[12,64]{0,1:T(8,128)S(1)} %get-tuple-element.126, f32[12,12]{1,0:T(8,128)S(1)} %get-tuple-element.125), kind=kOutput, calls=%fused_computation.5.clone.1 | convolution fusion | flops 117964800 | bytes 9440832 | tf_op jit(solution)/shard_map/while/body/eval_jaxpr/dot_general | solution.py:32
  139.8 4.0 %copy.91 = f32[12,64,1024]{2,1,0:T(8,128)S(1)} copy(f32[12,64,1024]{2,0,1:T(8,128)} %get-tuple-element.118) | data formatting | bytes 6291456 | tf_op jit(solution)/shard_map
  146.0 6.2 %add_divide_fusion.2 = f32[12,64,1024]{2,0,1:T(8,128)S(1)} fusion(f32[12,64,1024]{2,0,1:T(8,128)S(1)} %copy-done, f32[64,1024,12]{1,0,2:T(8,128)S(1)} %slice_bitcast_fusion.2, f32[12,64]{0,1:T(8,128)S(1)} %get-tuple-element.126, f32[12,12]{1,0:T(8,128)S(1)} %get-tuple-element.125), kind=kOutput, calls=%fused_computation.5.clone.1 | convolution fusion | flops 117964800 | bytes 9440832 | tf_op jit(solution)/shard_map/while/body/eval_jaxpr/dot_general | solution.py:32
  163.4 6.2 %add_divide_fusion.2 = f32[12,64,1024]{2,0,1:T(8,128)S(1)} fusion(f32[12,64,1024]{2,0,1:T(8,128)S(1)} %copy-done, f32[64,1024,12]{1,0,2:T(8,128)S(1)} %slice_bitcast_fusion.2, f32[12,64]{0,1:T(8,128)S(1)} %get-tuple-element.126, f32[12,12]{1,0:T(8,128)S(1)} %get-tuple-element.125), kind=kOutput, calls=%fused_computation.5.clone.1 | convolution fusion | flops 117964800 | bytes 9440832 | tf_op jit(solution)/shard_map/while/body/eval_jaxpr/dot_general | solution.py:32
  180.7 6.2 %add_divide_fusion.2 = f32[12,64,1024]{2,0,1:T(8,128)S(1)} fusion(f32[12,64,1024]{2,0,1:T(8,128)S(1)} %copy-done, f32[64,1024,12]{1,0,2:T(8,128)S(1)} %slice_bitcast_fusion.2, f32[12,64]{0,1:T(8,128)S(1)} %get-tuple-element.126, f32[12,12]{1,0:T(8,128)S(1)} %get-tuple-element.125), kind=kOutput, calls=%fused_computation.5.clone.1 | convolution fusion | flops 117964800 | bytes 9440832 | tf_op jit(solution)/shard_map/while/body/eval_jaxpr/dot_general | solution.py:32
  191.9 4.0 %copy.91 = f32[12,64,1024]{2,1,0:T(8,128)S(1)} copy(f32[12,64,1024]{2,0,1:T(8,128)} %get-tuple-element.118) | data formatting | bytes 6291456 | tf_op jit(solution)/shard_map
  198.1 6.2 %add_divide_fusion.2 = f32[12,64,1024]{2,0,1:T(8,128)S(1)} fusion(f32[12,64,1024]{2,0,1:T(8,128)S(1)} %copy-done, f32[64,1024,12]{1,0,2:T(8,128)S(1)} %slice_bitcast_fusion.2, f32[12,64]{0,1:T(8,128)S(1)} %get-tuple-element.126, f32[12,12]{1,0:T(8,128)S(1)} %get-tuple-element.125), kind=kOutput, calls=%fused_computation.5.clone.1 | convolution fusion | flops 117964800 | bytes 9440832 | tf_op jit(solution)/shard_map/while/body/eval_jaxpr/dot_general | solution.py:32
  209.3 4.0 %copy.91 = f32[12,64,1024]{2,1,0:T(8,128)S(1)} copy(f32[12,64,1024]{2,0,1:T(8,128)} %get-tuple-element.118) | data formatting | bytes 6291456 | tf_op jit(solution)/shard_map
  215.5 6.2 %add_divide_fusion.2 = f32[12,64,1024]{2,0,1:T(8,128)S(1)} fusion(f32[12,64,1024]{2,0,1:T(8,128)S(1)} %copy-done, f32[64,1024,12]{1,0,2:T(8,128)S(1)} %slice_bitcast_fusion.2, f32[12,64]{0,1:T(8,128)S(1)} %get-tuple-element.126, f32[12,12]{1,0:T(8,128)S(1)} %get-tuple-element.125), kind=kOutput, calls=%fused_computation.5.clone.1 | convolution fusion | flops 117964800 | bytes 9440832 | tf_op jit(solution)/shard_map/while/body/eval_jaxpr/dot_general | solution.py:32
  232.8 6.2 %add_divide_fusion.2 = f32[12,64,1024]{2,0,1:T(8,128)S(1)} fusion(f32[12,64,1024]{2,0,1:T(8,128)S(1)} %copy-done, f32[64,1024,12]{1,0,2:T(8,128)S(1)} %slice_bitcast_fusion.2, f32[12,64]{0,1:T(8,128)S(1)} %get-tuple-element.126, f32[12,12]{1,0:T(8,128)S(1)} %get-tuple-element.125), kind=kOutput, calls=%fused_computation.5.clone.1 | convolution fusion | flops 117964800 | bytes 9440832 | tf_op jit(solution)/shard_map/while/body/eval_jaxpr/dot_general | solution.py:32
  244.0 4.0 %copy.91 = f32[12,64,1024]{2,1,0:T(8,128)S(1)} copy(f32[12,64,1024]{2,0,1:T(8,128)} %get-tuple-element.118) | data formatting | bytes 6291456 | tf_op jit(solution)/shard_map
  250.2 6.2 %add_divide_fusion.2 = f32[12,64,1024]{2,0,1:T(8,128)S(1)} fusion(f32[12,64,1024]{2,0,1:T(8,128)S(1)} %copy-done, f32[64,1024,12]{1,0,2:T(8,128)S(1)} %slice_bitcast_fusion.2, f32[12,64]{0,1:T(8,128)S(1)} %get-tuple-element.126, f32[12,12]{1,0:T(8,128)S(1)} %get-tuple-element.125), kind=kOutput, calls=%fused_computation.5.clone.1 | convolution fusion | flops 117964800 | bytes 9440832 | tf_op jit(solution)/shard_map/while/body/eval_jaxpr/dot_general | solution.py:32
  267.5 6.2 %add_divide_fusion.2 = f32[12,64,1024]{2,0,1:T(8,128)S(1)} fusion(f32[12,64,1024]{2,0,1:T(8,128)S(1)} %copy-done, f32[64,1024,12]{1,0,2:T(8,128)S(1)} %slice_bitcast_fusion.2, f32[12,64]{0,1:T(8,128)S(1)} %get-tuple-element.126, f32[12,12]{1,0:T(8,128)S(1)} %get-tuple-element.125), kind=kOutput, calls=%fused_computation.5.clone.1 | convolution fusion | flops 117964800 | bytes 9440832 | tf_op jit(solution)/shard_map/while/body/eval_jaxpr/dot_general | solution.py:32
  278.7 4.0 %copy.91 = f32[12,64,1024]{2,1,0:T(8,128)S(1)} copy(f32[12,64,1024]{2,0,1:T(8,128)} %get-tuple-element.118) | data formatting | bytes 6291456 | tf_op jit(solution)/shard_map
  284.9 6.2 %add_divide_fusion.2 = f32[12,64,1024]{2,0,1:T(8,128)S(1)} fusion(f32[12,64,1024]{2,0,1:T(8,128)S(1)} %copy-done, f32[64,1024,12]{1,0,2:T(8,128)S(1)} %slice_bitcast_fusion.2, f32[12,64]{0,1:T(8,128)S(1)} %get-tuple-element.126, f32[12,12]{1,0:T(8,128)S(1)} %get-tuple-element.125), kind=kOutput, calls=%fused_computation.5.clone.1 | convolution fusion | flops 117964800 | bytes 9440832 | tf_op jit(solution)/shard_map/while/body/eval_jaxpr/dot_general | solution.py:32
  302.3 6.2 %add_divide_fusion.2 = f32[12,64,1024]{2,0,1:T(8,128)S(1)} fusion(f32[12,64,1024]{2,0,1:T(8,128)S(1)} %copy-done, f32[64,1024,12]{1,0,2:T(8,128)S(1)} %slice_bitcast_fusion.2, f32[12,64]{0,1:T(8,128)S(1)} %get-tuple-element.126, f32[12,12]{1,0:T(8,128)S(1)} %get-tuple-element.125), kind=kOutput, calls=%fused_computation.5.clone.1 | convolution fusion | flops 117964800 | bytes 9440832 | tf_op jit(solution)/shard_map/while/body/eval_jaxpr/dot_general | solution.py:32
  313.4 4.0 %copy.91 = f32[12,64,1024]{2,1,0:T(8,128)S(1)} copy(f32[12,64,1024]{2,0,1:T(8,128)} %get-tuple-element.118) | data formatting | bytes 6291456 | tf_op jit(solution)/shard_map
  319.6 6.2 %add_divide_fusion.2 = f32[12,64,1024]{2,0,1:T(8,128)S(1)} fusion(f32[12,64,1024]{2,0,1:T(8,128)S(1)} %copy-done, f32[64,1024,12]{1,0,2:T(8,128)S(1)} %slice_bitcast_fusion.2, f32[12,64]{0,1:T(8,128)S(1)} %get-tuple-element.126, f32[12,12]{1,0:T(8,128)S(1)} %get-tuple-element.125), kind=kOutput, calls=%fused_computation.5.clone.1 | convolution fusion | flops 117964800 | bytes 9440832 | tf_op jit(solution)/shard_map/while/body/eval_jaxpr/dot_general | solution.py:32
  337.0 6.2 %add_divide_fusion.2 = f32[12,64,1024]{2,0,1:T(8,128)S(1)} fusion(f32[12,64,1024]{2,0,1:T(8,128)S(1)} %copy-done, f32[64,1024,12]{1,0,2:T(8,128)S(1)} %slice_bitcast_fusion.2, f32[12,64]{0,1:T(8,128)S(1)} %get-tuple-element.126, f32[12,12]{1,0:T(8,128)S(1)} %get-tuple-element.125), kind=kOutput, calls=%fused_computation.5.clone.1 | convolution fusion | flops 117964800 | bytes 9440832 | tf_op jit(solution)/shard_map/while/body/eval_jaxpr/dot_general | solution.py:32
  348.1 4.0 %copy.91 = f32[12,64,1024]{2,1,0:T(8,128)S(1)} copy(f32[12,64,1024]{2,0,1:T(8,128)} %get-tuple-element.118) | data formatting | bytes 6291456 | tf_op jit(solution)/shard_map
  354.3 6.2 %add_divide_fusion.2 = f32[12,64,1024]{2,0,1:T(8,128)S(1)} fusion(f32[12,64,1024]{2,0,1:T(8,128)S(1)} %copy-done, f32[64,1024,12]{1,0,2:T(8,128)S(1)} %slice_bitcast_fusion.2, f32[12,64]{0,1:T(8,128)S(1)} %get-tuple-element.126, f32[12,12]{1,0:T(8,128)S(1)} %get-tuple-element.125), kind=kOutput, calls=%fused_computation.5.clone.1 | convolution fusion | flops 117964800 | bytes 9440832 | tf_op jit(solution)/shard_map/while/body/eval_jaxpr/dot_general | solution.py:32
  371.7 6.2 %add_divide_fusion.2 = f32[12,64,1024]{2,0,1:T(8,128)S(1)} fusion(f32[12,64,1024]{2,0,1:T(8,128)S(1)} %copy-done, f32[64,1024,12]{1,0,2:T(8,128)S(1)} %slice_bitcast_fusion.2, f32[12,64]{0,1:T(8,128)S(1)} %get-tuple-element.126, f32[12,12]{1,0:T(8,128)S(1)} %get-tuple-element.125), kind=kOutput, calls=%fused_computation.5.clone.1 | convolution fusion | flops 117964800 | bytes 9440832 | tf_op jit(solution)/shard_map/while/body/eval_jaxpr/dot_general | solution.py:32
  382.9 4.4 %fusion.11 = bf16[12,64,1024]{2,1,0:T(8,128)(2,1)S(1)} fusion(bf16[12,64,1024]{2,1,0:T(8,128)(2,1)} %copy-done.3, f32[12,64,1024]{2,0,1:T(8,128)} %get-tuple-element.32, pred[1024]{0:T(1024)(128)(4,1)S(1)} %copy-done.14), kind=kLoop, calls=%fused_computation.18 | loop fusion | flops 786432 | bytes 6292480 | tf_op jit(solution)/shard_map/jit(_where)/select_n | solution.py:87
  (234 shorter events, 217.1 us)
Async XLA Ops:
  0.0 6.3 %copy-start.12 = (bf16[64,8,128]{2,1,0:T(8,128)(2,1)S(1)}, bf16[64,8,128]{2,1,0:T(8,128)(2,1)}, u32[]{:S(2)}) copy-start(bf16[64,8,128]{2,1,0:T(8,128)(2,1)} %param.12) | copy-start | bytes 393220
  6.5 19.1 %copy-start.10 = (bf16[64,8,128]{2,1,0:T(8,128)(2,1)S(1)}, bf16[64,8,128]{2,1,0:T(8,128)(2,1)}, u32[]{:S(2)}) copy-start(bf16[64,8,128]{2,1,0:T(8,128)(2,1)} %param.11) | copy-start | bytes 393220
  15.9 40.5 %collective-permute-start.2 = (bf16[13,64,1,128]{3,1,2,0:T(8,128)(2,1)}, bf16[13,64,1,128]{3,1,2,0:T(8,128)(2,1)}, u32[]{:S(2)}, u32[]{:S(2)}) collective-permute-start(bf16[13,64,1,128]{3,1,2,0:T(8,128)(2,1)} %copy.65), channel_id=1, source_target_pairs={{0,1},{1,2},{2,3},{3,4},{4,5},{5,6},{6,7},{7,8},{8,9},{9,10},{10,1... | collective-permute-start | bytes 638984 | tf_op jit(solution)/shard_map/ppermute | solution.py:17
  23.3 36.2 %collective-permute-start.3 = (bf16[13,64,1,128]{3,1,2,0:T(8,128)(2,1)}, bf16[13,64,1,128]{3,1,2,0:T(8,128)(2,1)}, u32[]{:S(2)}, u32[]{:S(2)}) collective-permute-start(bf16[13,64,1,128]{3,1,2,0:T(8,128)(2,1)} %copy.66), channel_id=1, source_target_pairs={{1,0},{2,1},{3,2},{4,3},{5,4},{6,5},{7,6},{8,7},{9,8},{10,9},{11,1... | collective-permute-start | bytes 638984 | tf_op jit(solution)/shard_map/ppermute | solution.py:19
  28.2 26.7 %collective-permute-start = (bf16[13,64,8,1]{1,2,3,0:T(8,128)(2,1)}, bf16[13,64,8,1]{1,2,3,0:T(8,128)(2,1)S(1)}, u32[]{:S(2)}, u32[]{:S(2)}) collective-permute-start(bf16[13,64,8,1]{1,2,3,0:T(8,128)(2,1)} %get-tuple-element.78), channel_id=1, source_target_pairs={{0,16},{16,32},{32,48},{48,64},{64,80},{80,96},{96,112},{112,128},... | collective-permute-start | bytes 39944 | tf_op jit(solution)/shard_map/ppermute | solution.py:17
  30.5 24.4 %collective-permute-start.1 = (bf16[13,64,8,1]{1,2,3,0:T(8,128)(2,1)}, bf16[13,64,8,1]{1,2,3,0:T(8,128)(2,1)}, u32[]{:S(2)}, u32[]{:S(2)}) collective-permute-start(bf16[13,64,8,1]{1,2,3,0:T(8,128)(2,1)} %get-tuple-element.79), channel_id=1, source_target_pairs={{16,0},{32,16},{48,32},{64,48},{80,64},{96,80},{112,96},{128,112},... | collective-permute-start | bytes 39944 | tf_op jit(solution)/shard_map/ppermute | solution.py:19
  44.2 8.9 %copy-start.11 = (f32[64,8,128]{2,1,0:T(8,128)S(1)}, f32[64,8,128]{2,1,0:T(8,128)}, u32[]{:S(2)}) copy-start(f32[64,8,128]{2,1,0:T(8,128)} %get-tuple-element.75) | copy-start | bytes 786436
  62.3 7.3 %copy-start.6 = (f32[64,8,128]{0,1,2:T(8,128)S(1)}, f32[64,8,128]{0,1,2:T(8,128)}, u32[]{:S(2)}) copy-start(f32[64,8,128]{0,1,2:T(8,128)} %copy.60) | copy-start | bytes 786436
  62.3 7.3 %copy-start.7 = (f32[64,8,128]{0,1,2:T(8,128)S(1)}, f32[64,8,128]{0,1,2:T(8,128)}, u32[]{:S(2)}) copy-start(f32[64,8,128]{0,1,2:T(8,128)} %copy.69) | copy-start | bytes 786436
  62.3 7.3 %copy-start.8 = (f32[64,8,128]{0,1,2:T(8,128)S(1)}, f32[64,8,128]{0,1,2:T(8,128)}, u32[]{:S(2)}) copy-start(f32[64,8,128]{0,1,2:T(8,128)} %copy.54) | copy-start | bytes 786436
  62.3 7.3 %copy-start.9 = (f32[64,8,128]{0,1,2:T(8,128)S(1)}, f32[64,8,128]{0,1,2:T(8,128)}, u32[]{:S(2)}) copy-start(f32[64,8,128]{0,1,2:T(8,128)} %copy.59) | copy-start | bytes 786436
  79.2 3.2 copy-start.1
  79.2 3.2 copy-start.2
  79.2 3.2 copy-start.4
  79.2 3.3 copy-start.5
  101.2 3.9 %copy-start.13 = (f32[1,64,1]{1,2,0:T(1,128)S(1)}, f32[1,64,1]{1,2,0:T(1,128)}, u32[]{:S(2)}) copy-start(f32[1,64,1]{1,2,0:T(1,128)} %maximum_bitcast_fusion.2) | copy-start | bytes 772
  101.2 3.9 %copy-start.15 = (f32[12,12]{1,0:T(8,128)S(1)}, f32[12,12]{1,0:T(8,128)}, u32[]{:S(2)}) copy-start(f32[12,12]{1,0:T(8,128)} %param.14) | copy-start | bytes 1732
  102.1 2.9 copy-start.3
  105.1 277.8 %copy-start.14 = (pred[1024]{0:T(1024)(128)(4,1)S(1)}, pred[1024]{0:T(1024)(128)(4,1)}, u32[]{:S(2)}) copy-start(pred[1024]{0:T(1024)(128)(4,1)} %compare_bitcast_fusion) | copy-start | bytes 3076
  109.1 2.2 copy-start
  126.5 2.2 copy-start
  143.8 2.2 copy-start
  161.2 2.2 copy-start
  178.6 2.2 copy-start
  195.9 2.2 copy-start
  213.3 2.2 copy-start
  230.6 2.2 copy-start
  248.0 2.2 copy-start
  265.4 2.2 copy-start
  282.7 2.2 copy-start
  317.4 2.2 copy-start
  352.2 2.2 copy-start
  (3 other events, 6.6 us)
where the time goes:
time: 395 us; the launch traced here: 389 us
  local copies, waits for them, and re-layouts  166 us (42%)
  other arithmetic  114 us (29%)
  matrix products  98.6 us (25%)
  starting transfers between devices  9.1 us (2%)
    dot_general x16, matrix products, substep(): jnp.dot(coupling, state.reshape(species, levels * columns), precision=lax...  98.6 us
    another operation x16, local copies, waits for them, and re-layouts  64.2 us
    sub x16, other arithmetic, substep(): return state + flux - jnp.roll(flux, 1, axis=1)  55.4 us
    while x32, local copies, waits for them, and re-layouts  31.2 us
    add x3, other arithmetic, face_flux(): return jnp.maximum(speed, 0.0) * behind + jnp.minimum(speed, 0.0) * ahead  14.6 us
    mul x16, other arithmetic, substep(): flux = kappa_full * (jnp.roll(state, -1, axis=1) - state)  9.81 us
    slice x32, local copies, waits for them, and re-layouts, substep(): return state + flux - jnp.roll(flux, 1, axis=1)  9.09 us
  transfers between devices with their start and end apart: 4, of which 0 were waited for; matrix products, arithmetic and copies ran while one was open for 9% of the time, Pallas kernels for 0%

commit v1 on v0

v1 whole, which is shorter than its diff:
```python
import functools

import jax
import jax.numpy as jnp
from jax import lax
from jax.experimental import pallas as pl
from jax.experimental.pallas import tpu as pltpu
from jax.sharding import PartitionSpec as P

SUBSTEPS = 16
LANES = 128
LIT_CAP = 768
CHUNK = 128
NT = (((1,), (1,)), ((), ()))


def edge_kernel(species, levels, tr, east, north, lon_out, top_out, bottom_out, rows):
    lane = lax.broadcasted_iota(jnp.int32, (8, LANES), 1)
    for s in range(species + 1):
        packed = jnp.zeros((8, LANES), jnp.float32)
        for k in range(levels):
            if s < species:
                cell = tr[s * levels + k].astype(jnp.float32)
                rows[pl.ds((s * levels + k) * 8, 8), :] = cell
            else:
                cell = east[k].astype(jnp.float32)
                rows[pl.ds((s * levels + k) * 8, 8), :] = north[k].astype(jnp.float32)
            here = (lane == 2 * k) | (lane == (2 * k - 1) % LANES)
            moved = pltpu.roll(cell, 2 * k, 1) if k else cell
            packed = jnp.where(here, moved, packed)
        lon_out[s] = packed.astype(jnp.bfloat16)
    bottom_out[...] = rows[pl.ds(0, (species + 1) * levels, stride=8), :].astype(jnp.bfloat16)
    top_out[...] = rows[pl.ds(7, species * levels, stride=8), :].astype(jnp.bfloat16)


def main_kernel(
    species,
    levels,
    groups,
    pole,
    tr,
    east,
    north,
    lit,
    from_west,
    from_east,
    from_south,
    from_north,
    mix,
    loss,
    kappa,
    out,
    lon_edge,
    south_row,
    north_row,
    adv,
    xb,
    pick,
    state,
    made,
    back,
):
    f32, bf16 = jnp.float32, jnp.bfloat16
    lane = lax.broadcasted_iota(jnp.int32, (8, LANES), 1)
    sub = lax.broadcasted_iota(jnp.int32, (8, LANES), 0)
    width = groups * LANES

    for s in range(species + 1):
        lon_edge[s] = jnp.where(
            lane % 2 == 0, from_east[s].astype(f32), pltpu.roll(from_west[s].astype(f32), 2, 1)
        )
    south_row[...] = from_south[...].astype(f32)
    north_row[...] = from_north[...].astype(f32)
    at_pole = pole[0] > 0

    slots = LANES // species
    zero_tile = jnp.zeros((8, LANES), f32)
    for r in range(groups):
        for p in range(LANES):
            k = (p // species) * groups + r
            if p >= slots * species or k >= levels:
                adv[pl.ds((r * LANES + p) * 8, 8), :] = zero_tile

    def level(k, base):
        turn = LANES - 1 - 2 * k
        u = east[k].astype(f32)
        v = north[k].astype(f32)
        v = jnp.where(jnp.logical_and(at_pole, sub == 0), 0.0, v)
        u_next = jnp.where(
            lane == LANES - 1, pltpu.roll(lon_edge[species], turn, 1), pltpu.roll(u, LANES - 1, 1)
        )
        v_next = jnp.where(
            sub == 7, north_row[pl.ds(species * levels + k, 1), :], pltpu.roll(v, 7, 0)
        )
        a_west = jnp.maximum(u, 0.0)
        a_east = -jnp.minimum(u_next, 0.0)
        a_south = jnp.maximum(v, 0.0)
        a_north = -jnp.minimum(v_next, 0.0)
        a_here = (
            1.0
            - (jnp.maximum(u_next, 0.0) - jnp.minimum(u, 0.0))
            - (jnp.maximum(v_next, 0.0) - jnp.minimum(v, 0.0))
        )
        for s in range(species):
            c = tr[s * levels + k].astype(f32)
            edge = pltpu.roll(lon_edge[s], turn, 1)
            west = jnp.where(lane == 0, edge, pltpu.roll(c, 1, 1))
            east_c = jnp.where(lane == LANES - 1, edge, pltpu.roll(c, LANES - 1, 1))
            south = jnp.where(
                sub == 0, south_row[pl.ds(s * levels + k, 1), :], pltpu.roll(c, 1, 0)
            )
            north_c = jnp.where(
                sub == 7, north_row[pl.ds(s * levels + k, 1), :], pltpu.roll(c, 7, 0)
            )
            new = (
                a_here * c
                + a_west * west
                + a_east * east_c
                + a_south * south
                + a_north * north_c
            )
            at = pl.multiple_of((base + s) * 8, 8)
            adv[pl.ds(at, 8), :] = new.astype(bf16).astype(f32)

    whole_slots = levels // groups

    def slot_body(j, carry):
        for r in range(groups):
            level(j * groups + r, r * LANES + j * species)
        return carry

    lax.fori_loop(0, whole_slots, slot_body, 0)
    for r in range(levels - whole_slots * groups):
        level(whole_slots * groups + r, r * LANES + whole_slots * species)

    lit_mask = lit[...] > 0
    lit_f = lit_mask.astype(f32)
    upper = (
        lax.broadcasted_iota(jnp.int32, (LANES, LANES), 0)
        <= lax.broadcasted_iota(jnp.int32, (LANES, LANES), 1)
    ).astype(f32)
    lower = (
        lax.broadcasted_iota(jnp.int32, (8, 8), 0) > lax.broadcasted_iota(jnp.int32, (8, 8), 1)
    ).astype(f32)
    within = jnp.dot(lit_f, upper, preferred_element_type=f32)
    before = jnp.sum(jnp.dot(lower, lit_f, preferred_element_type=f32), axis=1, keepdims=True)
    rank = jnp.where(lit_mask, within + before - 1.0, -1.0).astype(jnp.int32)

    for j in range(8):
        order = lax.broadcasted_iota(jnp.int32, (LIT_CAP, LANES), 0)
        pick[:, j * LANES : (j + 1) * LANES] = (
            (order == rank[j : j + 1, :]).astype(f32).astype(bf16)
        )
        xb[:, j * LANES : (j + 1) * LANES] = adv[pl.ds(j, width, stride=8), :].astype(bf16)

    for r in range(0, groups, 2):
        n = min(2, groups - r)
        got = lax.dot_general(
            pick[...], xb[r * LANES : (r + n) * LANES, :], NT, preferred_element_type=f32
        )
        for i in range(n):
            state[r + i] = got[:, i * LANES : (i + 1) * LANES]

    def produce(parts, i):
        stack = []
        for q in parts:
            high = q.astype(bf16)
            low = (q - high.astype(f32)).astype(bf16)
            stack.append(jnp.concatenate([high, low], axis=1))
        res = jnp.dot(jnp.concatenate(stack, axis=0), mix[...], preferred_element_type=f32)
        for r in range(groups):
            part = res[r * CHUNK : (r + 1) * CHUNK]
            made[r, i * CHUNK : (i + 1) * CHUNK, :] = part[:, :LANES] + part[:, LANES:]

    def react(i):
        at = slice(i * CHUNK, (i + 1) * CHUNK)
        y = []
        for r in range(groups):
            q = state[r, at, :]
            lo = loss[r : r + 1, :]
            y.append(made[r, at, :] / ((1.0 + lo) + lo * (q * q)))
        flux = []
        for r in range(groups):
            if r + 1 < groups:
                above = y[r + 1]
            else:
                above = pltpu.roll(y[0], LANES - species, 1)
            flux.append(kappa[r : r + 1, :] * (above - y[r]))
        res = []
        for r in range(groups):
            below = flux[r - 1] if r else pltpu.roll(flux[groups - 1], species, 1)
            q = y[r] + flux[r] - below
            state[r, at, :] = q
            res.append(q)
        return res

    chunks = LIT_CAP // CHUNK
    for i in range(chunks):
        produce([state[r, i * CHUNK : (i + 1) * CHUNK, :] for r in range(groups)], i)

    def substep(step, carry):
        for i in range(chunks):
            produce(react(i), i)
        return carry

    lax.fori_loop(0, SUBSTEPS - 1, substep, 0)
    for i in range(chunks):
        for r, q in enumerate(react(i)):
            xb[r * LANES : (r + 1) * LANES, i * CHUNK : (i + 1) * CHUNK] = q.T.astype(bf16)

    for j in range(0, 8, 2):
        got = jnp.dot(
            xb[:, :LIT_CAP], pick[:, j * LANES : (j + 2) * LANES], preferred_element_type=f32
        )
        back[pl.ds(j, width, stride=8), :] = got[:, :LANES]
        back[pl.ds(j + 1, width, stride=8), :] = got[:, LANES:]

    def finish(k, base):
        for s in range(species):
            at = pl.multiple_of((base + s) * 8, 8)
            out[s * levels + k] = jnp.where(
                lit_mask, back[pl.ds(at, 8), :], adv[pl.ds(at, 8), :]
            ).astype(bf16)

    def finish_body(j, carry):
        for r in range(groups):
            finish(j * groups + r, r * LANES + j * species)
        return carry

    lax.fori_loop(0, whole_slots, finish_body, 0)
    for r in range(levels - whole_slots * groups):
        finish(whole_slots * groups + r, r * LANES + whole_slots * species)


def spread(values, species, slots, groups):
    levels = values.shape[1]
    full = jnp.pad(values, ((0, 0), (0, slots * groups - levels)))
    full = jnp.broadcast_to(full, (species, slots * groups))
    full = full.reshape(species, slots, groups).transpose(2, 1, 0).reshape(groups, slots * species)
    return jnp.pad(full, ((0, 8 - groups), (0, LANES - slots * species)))


def local(tracers, east_wind, north_wind, sunlit, coupling, rate_table, rate_index, kappa):
    species, levels, lat_rows, lon_cols = tracers.shape
    slots = LANES // species
    groups = -(-levels // slots)
    width = groups * LANES
    f32, bf16 = jnp.float32, jnp.bfloat16
    tr = tracers.reshape(species * levels, lat_rows, lon_cols)
    vmem = pl.BlockSpec(memory_space=pltpu.VMEM)
    lon_pack, top, bottom = pl.pallas_call(
        functools.partial(edge_kernel, species, levels),
        out_shape=(
            jax.ShapeDtypeStruct((species + 1, 8, LANES), bf16),
            jax.ShapeDtypeStruct((species * levels, LANES), bf16),
            jax.ShapeDtypeStruct(((species + 1) * levels, LANES), bf16),
        ),
        in_specs=[vmem] * 3,
        out_specs=(vmem,) * 3,
        scratch_shapes=[pltpu.VMEM(((species + 1) * levels * 8, LANES), f32)],
        name="edges",
    )(tr, east_wind, north_wind)

    nlon, nlat = lax.axis_size("lon"), lax.axis_size("lat")
    from_west = lax.ppermute(lon_pack, "lon", [(i, (i + 1) % nlon) for i in range(nlon)])
    from_east = lax.ppermute(lon_pack, "lon", [((i + 1) % nlon, i) for i in range(nlon)])
    from_south = lax.ppermute(top, "lat", [(i, i + 1) for i in range(nlat - 1)])
    from_north = lax.ppermute(bottom, "lat", [(i + 1, i) for i in range(nlat - 1)])

    rows = rate_table.shape[0]
    picker = (rate_index[:, None] == jnp.arange(rows, dtype=jnp.int32)[None, :]).astype(f32)
    loss = jnp.sum(picker[:, :, None] * rate_table[None, :, :], axis=1)
    loss = spread(loss, species, slots, groups)
    kap = spread(jnp.pad(kappa, (0, 1))[None], species, slots, groups)
    full = coupling.T + jnp.eye(species, dtype=f32)
    high = lax.reduce_precision(full, 8, 7)
    low = full - high
    row = jnp.arange(LANES)
    same = (row[:, None] // species == row[None, :] // species) & (row < slots * species)[None, :]

    def block(part):
        wide = jnp.pad(jnp.tile(part, (slots, slots)), ((0, LANES - slots * species),) * 2)
        return jnp.where(same, wide, 0.0)

    half = jnp.concatenate([block(high), block(low)], axis=1).astype(bf16)
    mix = jnp.concatenate([half, half], axis=0)
    pole = (lax.axis_index("lat") == 0).astype(jnp.int32).reshape(1)

    out = pl.pallas_call(
        functools.partial(main_kernel, species, levels, groups),
        out_shape=jax.ShapeDtypeStruct((species * levels, lat_rows, lon_cols), bf16),
        in_specs=[pl.BlockSpec(memory_space=pltpu.SMEM)] + [vmem] * 11,
        out_specs=vmem,
        scratch_shapes=[
            pltpu.VMEM((species + 1, 8, LANES), f32),
            pltpu.VMEM((species * levels, LANES), f32),
            pltpu.VMEM(((species + 1) * levels, LANES), f32),
            pltpu.VMEM((width * 8, LANES), f32),
            pltpu.VMEM((width, 8 * LANES), bf16),
            pltpu.VMEM((LIT_CAP, 8 * LANES), bf16),
            pltpu.VMEM((groups, LIT_CAP, LANES), f32),
            pltpu.VMEM((groups, LIT_CAP, LANES), f32),
            pltpu.VMEM((width * 8, LANES), f32),
        ],
        name="step",
    )(
        pole,
        tr,
        east_wind,
        north_wind,
        sunlit,
        from_west,
        from_east,
        from_south,
        from_north,
        mix,
        loss,
        kap,
    )
    return out.reshape(tracers.shape)


def solution(mesh):
    placed = (
        P(None, None, "lat", "lon"),
        P(None, "lat", "lon"),
        P(None, "lat", "lon"),
        P("lat", "lon"),
        P(),
        P(),
        P(),
        P(),
    )
    return jax.shard_map(
        local, mesh=mesh, in_specs=placed, out_specs=P(None, None, "lat", "lon"), check_vma=False
    )
```

time: 395 us -> 57.8 us (0.15)
  the two profiles are of different devices: /device:TPU:113 before, /device:TPU:123 now
where the time goes in v1:
time: 57.8 us; the launch traced here: 57.6 us
  Pallas kernels  36.7 us (63%)
  starting transfers between devices  9.18 us (16%)
  waiting for transfers between devices  7.15 us (12%)
  local copies, waits for them, and re-layouts  3.45 us (6%)
  other arithmetic  0.94 us (2%)
    pallas_call x1, Pallas kernels, local(): pl.pallas_call(functools.partial(main_kernel, species, levels, groups), o...  33.9 us
    ppermute x1, waiting for transfers between devices, local(): lax.ppermute(bottom, 'lat', [(i + 1, i) for i in range(nlat - 1)])  7.14 us
    ppermute x1, starting transfers between devices, local(): from_south = lax.ppermute(top, 'lat', [(i, i + 1) for i in range(nlat - 1)])  5.42 us
    pallas_call x1, Pallas kernels, local(): pl.pallas_call(functools.partial(edge_kernel, species, levels), out_shape...  2.84 us
    ppermute x1, starting transfers between devices, local(): lax.ppermute(bottom, 'lat', [(i + 1, i) for i in range(nlat - 1)])  1.92 us
    pad x2, local copies, waits for them, and re-layouts, spread(): return jnp.pad(full, ((0, 8 - groups), (0, LANES - slots * species)))  1.19 us
    ppermute x1, starting transfers between devices, local(): lax.ppermute(lon_pack, 'lon', [(i, (i + 1) % nlon) for i in range(nlon)])  1.17 us
  transfers between devices with their start and end apart: 4, of which 1 were waited for; matrix products, arithmetic and copies ran while one was open for 6% of the time, Pallas kernels for 0%

profile of v1, /device:TPU:123, one launch (start us, length us, event | category | flops | bytes accessed | tf_op | source)
XLA Modules:
  0.0 57.6 jit_solution(9470844720252161692)
XLA Ops:
  0.0 2.8 %edges.1 = (bf16[13,8,128]{2,1,0:T(8,128)(2,1)}, bf16[768,128]{1,0:T(8,128)(2,1)}, bf16[832,128]{1,0:T(8,128)(2,1)}) custom-call(bf16[768,8,128]{2,1,0:T(8,128)(2,1)} %bitcast.18, bf16[64,8,128]{2,1,0:T(8,128)(2,1)} %east.3, bf16[64,8,128]{2,1,0:T(8,128)(2,1)} %north.3), custom_call_target="tpu_custom_call" | custom-call | tf_op jit(solution)/shard_map/edges/pallas_call | solution.py:251
  2.9 0.7 %collective-permute-start.1 = (bf16[13,8,128]{2,1,0:T(8,128)(2,1)}, bf16[13,8,128]{2,1,0:T(8,128)(2,1)S(1)}, u32[]{:S(2)}, u32[]{:S(2)}) collective-permute-start(bf16[13,8,128]{2,1,0:T(8,128)(2,1)} %get-tuple-element.8), channel_id=1, source_target_pairs={{16,0},{32,16},{48,32},{64,48},{80,64},{96,80},{112,96},{128,112},... | collective-permute-start | bytes 79880 | tf_op jit(solution)/shard_map/ppermute | solution.py:266
  3.5 1.2 %collective-permute-start = (bf16[13,8,128]{2,1,0:T(8,128)(2,1)}, bf16[13,8,128]{2,1,0:T(8,128)(2,1)S(1)}, u32[]{:S(2)}, u32[]{:S(2)}) collective-permute-start(bf16[13,8,128]{2,1,0:T(8,128)(2,1)} %get-tuple-element.8), channel_id=1, source_target_pairs={{0,16},{16,32},{32,48},{48,64},{64,80},{80,96},{96,112},{112,128},... | collective-permute-start | bytes 79880 | tf_op jit(solution)/shard_map/ppermute | solution.py:265
  4.7 5.4 %collective-permute-start.2 = (bf16[768,128]{1,0:T(8,128)(2,1)}, bf16[768,128]{1,0:T(8,128)(2,1)S(1)}, u32[]{:S(2)}, u32[]{:S(2)}) collective-permute-start(bf16[768,128]{1,0:T(8,128)(2,1)} %get-tuple-element.9), channel_id=1, source_target_pairs={{0,1},{1,2},{2,3},{3,4},{4,5},{5,6},{6,7},{7,8},{8,9},{9,10},{10,1... | collective-permute-start | bytes 589832 | tf_op jit(solution)/shard_map/ppermute | solution.py:267
  10.1 1.9 %collective-permute-start.3 = (bf16[832,128]{1,0:T(8,128)(2,1)}, bf16[832,128]{1,0:T(8,128)(2,1)S(1)}, u32[]{:S(2)}, u32[]{:S(2)}) collective-permute-start(bf16[832,128]{1,0:T(8,128)(2,1)} %get-tuple-element.10), channel_id=1, source_target_pairs={{1,0},{2,1},{3,2},{4,3},{5,4},{6,5},{7,6},{8,7},{9,8},{10,9},{11,1... | collective-permute-start | bytes 638984 | tf_op jit(solution)/shard_map/ppermute | solution.py:268
  12.1 0.0 copy-done.7
  12.1 0.1 broadcast_in_dim.24
  12.2 0.1 copy.20
  12.3 0.0 copy-done.6
  12.3 0.1 fusion
  12.4 0.1 copy.16
  12.5 0.1 copy.17
  12.6 0.1 broadcast_bitcast_fusion
  12.7 0.1 tile.20
  12.8 0.3 tile.21
  13.1 0.1 tile.8
  13.2 0.3 tile.9
  13.5 0.1 select_convert_fusion.1
  13.6 0.1 multiply_reduce_fusion
  13.7 0.7 %maximum_maximum_fusion.mix = bf16[256,256]{1,0:T(8,128)(2,1)} fusion(bf16[128,128]{1,0:T(8,128)(2,1)S(1)} %get-tuple-element.14, bf16[128,128]{1,0:T(8,128)(2,1)S(1)} %get-tuple-element.13), kind=kLoop, calls=%fused_computation | loop fusion | flops 524288 | bytes 196608 | tf_op jit(solution)/shard_map/concatenate | solution.py:286
  14.3 0.1 copy.21
  14.5 0.1 reshape.105
  14.6 0.6 %pad.29.loss = f32[8,128]{1,0:T(8,128)} pad(f32[7,120]{1,0:T(8,128)S(1)} %reshape.105, f32[]{:T(128)} %constant.25.clone.1), padding=0_1x0_8 | pad | bytes 7460 | tf_op jit(solution)/shard_map/jit(_pad)/pad | solution.py:240
  15.2 0.1 reshape.106
  15.2 0.6 %pad.32.kappa = f32[8,128]{1,0:T(8,128)} pad(f32[7,120]{1,0:T(8,128)S(1)} %reshape.106, f32[]{:T(128)} %constant.25.clone.1), padding=0_1x0_8 | pad | bytes 7460 | tf_op jit(solution)/shard_map/jit(_pad)/pad | solution.py:240
  15.8 0.0 collective-permute-done.1.from_east
  15.8 0.0 collective-permute-done.from_west
  15.9 0.0 collective-permute-done.2.from_south
  15.9 7.1 %collective-permute-done.3.from_north = bf16[832,128]{1,0:T(8,128)(2,1)S(1)} collective-permute-done((bf16[832,128]{1,0:T(8,128)(2,1)}, bf16[832,128]{1,0:T(8,128)(2,1)S(1)}, u32[]{:S(2)}, u32[]{:S(2)}) %collective-permute-start.3) | collective-permute-done | bytes 213024 | tf_op jit(solution)/shard_map/ppermute | solution.py:268
  23.0 0.0 copy-done.3
  23.0 0.7 %copy-done = bf16[832,128]{1,0:T(8,128)(2,1)} copy-done((bf16[832,128]{1,0:T(8,128)(2,1)}, bf16[832,128]{1,0:T(8,128)(2,1)S(1)}, u32[]{:S(2)}) %copy-start) | copy-done | bytes 213016
  23.7 33.9 %step.1 = bf16[768,8,128]{2,1,0:T(8,128)(2,1)} custom-call(s32[1]{0:T(128)} %bitcast.pole, bf16[768,8,128]{2,1,0:T(8,128)(2,1)} %bitcast.19, bf16[64,8,128]{2,1,0:T(8,128)(2,1)} %east.3, bf16[64,8,128]{2,1,0:T(8,128)(2,1)} %north.3, s32[8,128]{1,0:T(8,128)} %lit.1, bf16[13,8,128]{2,1,0:T(8,128)(2,1)} %copy-done.3, bf16[13,8,128]{2,1,0:T(8,128)(2,1)} %copy-done.2, ...), custom_call_target="tpu_custom_call" | custom-call | tf_op jit(solution)/shard_map/step/pallas_call | solution.py:289
  (20 shorter events, 0.1 us)
Async XLA Ops:
  0.0 12.1 %copy-start.7 = (f32[63]{0:T(128)S(1)}, f32[63]{0:T(128)}, u32[]{:S(2)}) copy-start(f32[63]{0:T(128)} %param.15) | copy-start | bytes 760
  0.0 12.3 %copy-start.6 = (s32[12]{0:T(128)S(1)}, s32[12]{0:T(128)}, u32[]{:S(2)}) copy-start(s32[12]{0:T(128)} %param.14) | copy-start | bytes 148
  0.0 12.4 %copy-start.4 = (f32[12,12]{1,0:T(8,128)S(1)}, f32[12,12]{1,0:T(8,128)}, u32[]{:S(2)}) copy-start(f32[12,12]{1,0:T(8,128)} %param.12) | copy-start | bytes 1732
  2.8 10.7 %copy-start.5 = (f32[8,64]{1,0:T(8,128)S(1)}, f32[8,64]{1,0:T(8,128)}, u32[]{:S(2)}) copy-start(f32[8,64]{1,0:T(8,128)} %param.13) | copy-start | bytes 6148
  2.9 13.0 %collective-permute-start.1 = (bf16[13,8,128]{2,1,0:T(8,128)(2,1)}, bf16[13,8,128]{2,1,0:T(8,128)(2,1)S(1)}, u32[]{:S(2)}, u32[]{:S(2)}) collective-permute-start(bf16[13,8,128]{2,1,0:T(8,128)(2,1)} %get-tuple-element.8), channel_id=1, source_target_pairs={{16,0},{32,16},{48,32},{64,48},{80,64},{96,80},{112,96},{128,112},... | collective-permute-start | bytes 79880 | tf_op jit(solution)/shard_map/ppermute | solution.py:266
  3.5 12.3 %collective-permute-start = (bf16[13,8,128]{2,1,0:T(8,128)(2,1)}, bf16[13,8,128]{2,1,0:T(8,128)(2,1)S(1)}, u32[]{:S(2)}, u32[]{:S(2)}) collective-permute-start(bf16[13,8,128]{2,1,0:T(8,128)(2,1)} %get-tuple-element.8), channel_id=1, source_target_pairs={{0,16},{16,32},{32,48},{48,64},{64,80},{80,96},{96,112},{112,128},... | collective-permute-start | bytes 79880 | tf_op jit(solution)/shard_map/ppermute | solution.py:265
  4.7 11.2 %collective-permute-start.2 = (bf16[768,128]{1,0:T(8,128)(2,1)}, bf16[768,128]{1,0:T(8,128)(2,1)S(1)}, u32[]{:S(2)}, u32[]{:S(2)}) collective-permute-start(bf16[768,128]{1,0:T(8,128)(2,1)} %get-tuple-element.9), channel_id=1, source_target_pairs={{0,1},{1,2},{2,3},{3,4},{4,5},{5,6},{6,7},{7,8},{8,9},{9,10},{10,1... | collective-permute-start | bytes 589832 | tf_op jit(solution)/shard_map/ppermute | solution.py:267
  10.1 12.9 %collective-permute-start.3 = (bf16[832,128]{1,0:T(8,128)(2,1)}, bf16[832,128]{1,0:T(8,128)(2,1)S(1)}, u32[]{:S(2)}, u32[]{:S(2)}) collective-permute-start(bf16[832,128]{1,0:T(8,128)(2,1)} %get-tuple-element.10), channel_id=1, source_target_pairs={{1,0},{2,1},{3,2},{4,3},{5,4},{6,5},{7,6},{8,7},{9,8},{10,9},{11,1... | collective-permute-start | bytes 638984 | tf_op jit(solution)/shard_map/ppermute | solution.py:268
  15.8 7.2 %copy-start.2 = (bf16[13,8,128]{2,1,0:T(8,128)(2,1)}, bf16[13,8,128]{2,1,0:T(8,128)(2,1)S(1)}, u32[]{:S(2)}) copy-start(bf16[13,8,128]{2,1,0:T(8,128)(2,1)S(1)} %collective-permute-done.1.from_east) | copy-start | bytes 79876
  15.8 7.2 %copy-start.3 = (bf16[13,8,128]{2,1,0:T(8,128)(2,1)}, bf16[13,8,128]{2,1,0:T(8,128)(2,1)S(1)}, u32[]{:S(2)}) copy-start(bf16[13,8,128]{2,1,0:T(8,128)(2,1)S(1)} %collective-permute-done.from_west) | copy-start | bytes 79876
  15.9 7.2 %copy-start.1 = (bf16[768,128]{1,0:T(8,128)(2,1)}, bf16[768,128]{1,0:T(8,128)(2,1)S(1)}, u32[]{:S(2)}) copy-start(bf16[768,128]{1,0:T(8,128)(2,1)S(1)} %collective-permute-done.2.from_south) | copy-start | bytes 589828
  23.0 0.7 %copy-start = (bf16[832,128]{1,0:T(8,128)(2,1)}, bf16[832,128]{1,0:T(8,128)(2,1)S(1)}, u32[]{:S(2)}) copy-start(bf16[832,128]{1,0:T(8,128)(2,1)S(1)} %collective-permute-done.3.from_north) | copy-start | bytes 638980

commit v2 on v0

v2 whole, which is shorter than its diff:
```python
import functools

import jax
import jax.numpy as jnp
from jax import lax
from jax.experimental import pallas as pl
from jax.experimental.pallas import tpu as pltpu
from jax.sharding import PartitionSpec as P

SUBSTEPS = 16
LANES = 128
LIT_CAP = 768
FIRST = 512
CHUNK = 64
VMEM_LIMIT = 24 << 20
NT = (((1,), (1,)), ((), ()))
f32, bf16 = jnp.float32, jnp.bfloat16


def iota(shape, axis):
    return lax.broadcasted_iota(jnp.int32, shape, axis)


def place(k, s, species, groups):
    return (k % groups) * LANES + (k // groups) * species + s


def edge_kernel(species, levels, groups, tr, east, north, lon_out, top_out, bottom_out, rows, vrow):
    lane = iota((8, LANES), 1)
    zero = jnp.zeros((8, LANES), f32)
    for r in range(groups):
        for p in range(LANES):
            if p >= (LANES // species) * species or (p // species) * groups + r >= levels:
                rows[pl.ds((r * LANES + p) * 8, 8), :] = zero
    for s in range(species + 1):
        packed = zero
        for k in range(levels):
            if s < species:
                cell = tr[s * levels + k].astype(f32)
                rows[pl.ds(place(k, s, species, groups) * 8, 8), :] = cell
            else:
                cell = east[k].astype(f32)
                vrow[pl.ds(k * 8, 8), :] = north[k].astype(f32)
            here = (lane == 2 * k) | (lane == (2 * k - 1) % LANES)
            moved = pltpu.roll(cell, 2 * k, 1) if k else cell
            packed = jnp.where(here, moved, packed)
        lon_out[s] = packed.astype(bf16)
    width = groups * LANES
    bottom_out[:width] = rows[pl.ds(0, width, stride=8), :].astype(bf16)
    bottom_out[width:] = vrow[pl.ds(0, levels, stride=8), :].astype(bf16)
    top_out[...] = rows[pl.ds(7, width, stride=8), :].astype(bf16)


def run_chemistry(groups, species, count, mix, loss, kappa, state, made, emit):
    def produce(parts, i):
        stack = []
        for q in parts:
            high = q.astype(bf16)
            low = (q - high.astype(f32)).astype(bf16)
            stack.append(jnp.concatenate([high, low], axis=1))
        res = jnp.dot(jnp.concatenate(stack, axis=0), mix[...], preferred_element_type=f32)
        for r in range(groups):
            part = res[r * CHUNK : (r + 1) * CHUNK]
            made[r, i * CHUNK : (i + 1) * CHUNK, :] = part[:, :LANES] + part[:, LANES:]

    def react(i):
        at = slice(i * CHUNK, (i + 1) * CHUNK)
        y = []
        for r in range(groups):
            q = state[r, at, :]
            lo = loss[r : r + 1, :]
            y.append(made[r, at, :] / ((1.0 + lo) + lo * (q * q)))
        flux = []
        for r in range(groups):
            if r + 1 < groups:
                above = y[r + 1]
            else:
                above = pltpu.roll(y[0], LANES - species, 1)
            flux.append(kappa[r : r + 1, :] * (above - y[r]))
        res = []
        for r in range(groups):
            below = flux[r - 1] if r else pltpu.roll(flux[groups - 1], species, 1)
            q = y[r] + flux[r] - below
            state[r, at, :] = q
            res.append(q)
        return res

    chunks = count // CHUNK
    for i in range(chunks):
        produce([state[r, i * CHUNK : (i + 1) * CHUNK, :] for r in range(groups)], i)

    def substep(step, carry):
        for i in range(chunks):
            produce(react(i), i)
        return carry

    lax.fori_loop(0, SUBSTEPS - 1, substep, 0)
    for i in range(chunks):
        react(i)
    for r in range(groups):
        emit(r, state[r, :count, :].T.astype(bf16))


def tables(species, levels, groups, coupling, rate_table, rate_index, kappa, mix, tab, loss_rows):
    slots = LANES // species
    for s in range(species):
        loss_rows[s : s + 1, :] = rate_table[pl.ds(rate_index[s], 1), :]
    p = iota((LANES, species), 0)
    slot = (p * 171) >> 11
    spread = jnp.logical_and(p - slot * species == iota((LANES, species), 1), slot < slots)
    spread = spread.astype(f32)
    full = coupling[...] + (iota((species, species), 0) == iota((species, species), 1)).astype(f32)
    same = ((iota((LANES, LANES), 0) * 171) >> 11) == ((iota((LANES, LANES), 1) * 171) >> 11)

    def block(part):
        half = lax.dot_general(spread, part.astype(f32), NT, preferred_element_type=f32)
        wide = lax.dot_general(half, spread, NT, preferred_element_type=f32)
        return jnp.where(same, wide, 0.0).astype(bf16)

    high = full.astype(bf16)
    low = (full - high.astype(f32)).astype(bf16)
    for at in (0, LANES):
        mix[at : at + LANES, :LANES] = block(high)
        mix[at : at + LANES, LANES:] = block(low)
    width = groups * LANES
    col = iota((levels, width), 1)
    lane = col & (LANES - 1)
    slot = (lane * 171) >> 11
    sel = jnp.logical_and(iota((levels, width), 0) == slot * groups + (col >> 7), slot < slots)
    sel = sel.astype(f32)
    exact = lax.Precision.HIGHEST
    spread_loss = jnp.dot(loss_rows[...], sel, preferred_element_type=f32, precision=exact)
    col = iota((species, width), 1) & (LANES - 1)
    mine = col - ((col * 171) >> 11) * species == iota((species, width), 0)
    loss = jnp.sum(jnp.where(mine, spread_loss, 0.0), axis=0, keepdims=True)
    kap = jnp.dot(kappa[...], sel, preferred_element_type=f32, precision=exact)
    for r in range(groups):
        tab[r : r + 1, :] = loss[:, r * LANES : (r + 1) * LANES]
        tab[8 + r : 9 + r, :] = kap[:, r * LANES : (r + 1) * LANES]


def first_kernel(
    species,
    levels,
    groups,
    pole,
    rate_index,
    tr,
    east,
    north,
    lit,
    from_west,
    from_east,
    coupling,
    rate_table,
    kappa,
    part_out,
    xb,
    pick,
    fin,
    mix,
    tab,
    lon_edge,
    adv,
    state,
    made,
    loss_rows,
):
    lane = iota((8, LANES), 1)
    sub = iota((8, LANES), 0)
    width = groups * LANES
    slots = LANES // species

    tables(species, levels, groups, coupling, rate_table, rate_index, kappa, mix, tab, loss_rows)
    for s in range(species + 1):
        lon_edge[s] = jnp.where(
            lane % 2 == 0, from_east[s].astype(f32), pltpu.roll(from_west[s].astype(f32), 2, 1)
        )
    at_pole = pole[0] > 0

    zero_tile = jnp.zeros((8, LANES), f32)
    for r in range(groups):
        for p in range(LANES):
            if p >= slots * species or (p // species) * groups + r >= levels:
                adv[pl.ds((r * LANES + p) * 8, 8), :] = zero_tile

    def level(k, base):
        turn = LANES - 1 - 2 * k
        u = east[k].astype(f32)
        v = north[k].astype(f32)
        v = jnp.where(jnp.logical_and(at_pole, sub == 0), 0.0, v)
        u_next = jnp.where(
            lane == LANES - 1, pltpu.roll(lon_edge[species], turn, 1), pltpu.roll(u, LANES - 1, 1)
        )
        v_next = jnp.where(sub == 7, 0.0, pltpu.roll(v, 7, 0))
        a_west = jnp.maximum(u, 0.0)
        a_east = -jnp.minimum(u_next, 0.0)
        a_south = jnp.where(sub == 0, 0.0, jnp.maximum(v, 0.0))
        a_north = -jnp.minimum(v_next, 0.0)
        a_here = (
            1.0
            - (jnp.maximum(u_next, 0.0) - jnp.minimum(u, 0.0))
            - (jnp.maximum(v_next, 0.0) - jnp.minimum(v, 0.0))
        )
        for s in range(species):
            c = tr[s * levels + k].astype(f32)
            edge = pltpu.roll(lon_edge[s], turn, 1)
            west = jnp.where(lane == 0, edge, pltpu.roll(c, 1, 1))
            east_c = jnp.where(lane == LANES - 1, edge, pltpu.roll(c, LANES - 1, 1))
            new = (
                a_here * c
                + a_west * west
                + a_east * east_c
                + a_south * pltpu.roll(c, 1, 0)
                + a_north * pltpu.roll(c, 7, 0)
            )
            at = pl.multiple_of((base + s) * 8, 8)
            adv[pl.ds(at, 8), :] = new

    whole_slots = levels // groups

    def slot_body(j, carry):
        for r in range(groups):
            level(j * groups + r, r * LANES + j * species)
        return carry

    lax.fori_loop(0, whole_slots, slot_body, 0)
    for r in range(levels - whole_slots * groups):
        level(whole_slots * groups + r, r * LANES + whole_slots * species)

    lit_mask = lit[...] > 0
    inner = jnp.logical_and(sub > 0, sub < 7)
    upper = (iota((LANES, LANES), 0) <= iota((LANES, LANES), 1)).astype(f32)
    lower = (iota((8, 8), 0) > iota((8, 8), 1)).astype(f32)

    def rank_of(mask):
        ones = mask.astype(f32)
        within = jnp.dot(ones, upper, preferred_element_type=f32)
        before = jnp.sum(jnp.dot(lower, ones, preferred_element_type=f32), axis=1, keepdims=True)
        return within + before - 1.0

    inner_rank = rank_of(jnp.logical_and(lit_mask, inner))
    outer_lit = jnp.logical_and(lit_mask, jnp.logical_not(inner))
    outer_rank = rank_of(outer_lit)
    outer_count = jnp.sum(outer_lit.astype(f32))
    slot = jnp.where(
        inner,
        inner_rank + jnp.where(inner_rank >= FIRST, outer_count, 0.0),
        outer_rank + FIRST,
    )
    slot = jnp.where(lit_mask, slot, -1.0).astype(jnp.int32)

    order = iota((LIT_CAP, LANES), 0)
    for j in range(8):
        pick[:, j * LANES : (j + 1) * LANES] = (
            (order == slot[j : j + 1, :]).astype(f32).astype(bf16)
        )
        rows = adv[pl.ds(j, width, stride=8), :]
        if 0 < j < 7:
            xb[:, j * LANES : (j + 1) * LANES] = rows.astype(bf16)
        else:
            xb[:, j * LANES : (j + 1) * LANES] = jnp.zeros((width, LANES), bf16)
            part_out[j // 7] = rows

    span = slice(LANES, 7 * LANES)
    for r in range(0, groups, 2):
        n = min(2, groups - r)
        got = lax.dot_general(
            pick[:FIRST, span],
            xb[r * LANES : (r + n) * LANES, span],
            NT,
            preferred_element_type=f32,
        )
        for i in range(n):
            state[r + i] = got[:, i * LANES : (i + 1) * LANES]

    def emit(r, value):
        fin[r * LANES : (r + 1) * LANES, :] = value

    run_chemistry(groups, species, FIRST, mix, tab, tab.at[8:16], state, made, emit)


def second_kernel(
    species,
    levels,
    groups,
    pole,
    part,
    top,
    bottom,
    from_south,
    from_north,
    xb,
    pick,
    fin,
    mix,
    tab,
    lit,
    out,
    xe,
    fin_b,
    state,
    made,
    back,
):
    width = groups * LANES
    slots = LANES // species
    lit_mask = lit[...] > 0
    row = iota((width, levels), 0)
    slot = ((row & (LANES - 1)) * 171) >> 11
    sel = jnp.logical_and(iota((width, levels), 1) == slot * groups + (row >> 7), slot < slots)
    sel = sel.astype(f32).astype(bf16)
    v_here = jnp.dot(sel, bottom[width:, :], preferred_element_type=f32)
    v_here = jnp.where(pole[0] > 0, 0.0, jnp.maximum(v_here, 0.0))
    xe[:, :LANES] = (part[0] + v_here * from_south[...].astype(f32)).astype(bf16)
    v_next = jnp.dot(sel, from_north[width:, :], preferred_element_type=f32)
    xe[:, LANES:] = (
        part[1]
        - jnp.maximum(v_next, 0.0) * top[...].astype(f32)
        - jnp.minimum(v_next, 0.0) * from_north[:width, :].astype(f32)
    ).astype(bf16)

    rest = slice(FIRST, LIT_CAP)
    span = slice(LANES, 7 * LANES)
    for r in range(0, groups, 2):
        n = min(2, groups - r)
        rows = slice(r * LANES, (r + n) * LANES)
        got = lax.dot_general(pick[rest, span], xb[rows, span], NT, preferred_element_type=f32)
        got = got + lax.dot_general(
            pick[rest, :LANES], xe[rows, :LANES], NT, preferred_element_type=f32
        )
        got = got + lax.dot_general(
            pick[rest, 7 * LANES :], xe[rows, LANES:], NT, preferred_element_type=f32
        )
        for i in range(n):
            state[r + i] = got[:, i * LANES : (i + 1) * LANES]

    def emit(r, value):
        fin_b[r * LANES : (r + 1) * LANES, :] = value

    run_chemistry(groups, species, LIT_CAP - FIRST, mix, tab, tab.at[8:16], state, made, emit)

    def settle(j, got, moved):
        keep = lit_mask[j : j + 1, :]
        back[pl.ds(j, width, stride=8), :] = jnp.where(keep, got, moved.astype(f32))

    for j in range(1, 7, 2):
        cols = slice(j * LANES, (j + 2) * LANES)
        got = jnp.dot(fin[...], pick[:FIRST, cols], preferred_element_type=f32)
        got = got + jnp.dot(fin_b[...], pick[rest, cols], preferred_element_type=f32)
        settle(j, got[:, :LANES], xb[:, j * LANES : (j + 1) * LANES])
        settle(j + 1, got[:, LANES:], xb[:, (j + 1) * LANES : (j + 2) * LANES])
    for i, j in enumerate((0, 7)):
        got = jnp.dot(
            fin_b[...], pick[rest, j * LANES : (j + 1) * LANES], preferred_element_type=f32
        )
        settle(j, got, xe[:, i * LANES : (i + 1) * LANES])

    def finish(k, base):
        for s in range(species):
            at = pl.multiple_of((base + s) * 8, 8)
            out[s * levels + k] = back[pl.ds(at, 8), :].astype(bf16)

    whole_slots = levels // groups

    def finish_body(j, carry):
        for r in range(groups):
            finish(j * groups + r, r * LANES + j * species)
        return carry

    lax.fori_loop(0, whole_slots, finish_body, 0)
    for r in range(levels - whole_slots * groups):
        finish(whole_slots * groups + r, r * LANES + whole_slots * species)


def local(tracers, east_wind, north_wind, sunlit, coupling, rate_table, rate_index, kappa):
    species, levels, lat_rows, lon_cols = tracers.shape
    slots = LANES // species
    groups = -(-levels // slots)
    width = groups * LANES
    sizes = (species, levels, groups)
    tr = tracers.reshape(species * levels, lat_rows, lon_cols)
    vmem = pl.BlockSpec(memory_space=pltpu.VMEM)
    smem = pl.BlockSpec(memory_space=pltpu.SMEM)
    shape = jax.ShapeDtypeStruct
    lon_pack, top, bottom = pl.pallas_call(
        functools.partial(edge_kernel, *sizes),
        out_shape=(
            shape((species + 1, 8, LANES), bf16),
            shape((width, LANES), bf16),
            shape((width + levels, LANES), bf16),
        ),
        in_specs=[vmem] * 3,
        out_specs=(vmem,) * 3,
        scratch_shapes=[pltpu.VMEM((width * 8, LANES), f32), pltpu.VMEM((levels * 8, LANES), f32)],
        name="edges",
    )(tr, east_wind, north_wind)

    nlon, nlat = lax.axis_size("lon"), lax.axis_size("lat")
    from_south = lax.ppermute(top, "lat", [(i, i + 1) for i in range(nlat - 1)])
    from_north = lax.ppermute(bottom, "lat", [(i + 1, i) for i in range(nlat - 1)])
    from_west = lax.ppermute(lon_pack, "lon", [(i, (i + 1) % nlon) for i in range(nlon)])
    from_east = lax.ppermute(lon_pack, "lon", [((i + 1) % nlon, i) for i in range(nlon)])
    pole = (lax.axis_index("lat") == 0).astype(jnp.int32).reshape(1)

    part, xb, pick, fin, mix, tab = pl.pallas_call(
        functools.partial(first_kernel, *sizes),
        out_shape=(
            shape((2, width, LANES), f32),
            shape((width, 8 * LANES), bf16),
            shape((LIT_CAP, 8 * LANES), bf16),
            shape((width, FIRST), bf16),
            shape((2 * LANES, 2 * LANES), bf16),
            shape((16, LANES), f32),
        ),
        in_specs=[smem] * 2 + [vmem] * 9,
        out_specs=(vmem,) * 6,
        scratch_shapes=[
            pltpu.VMEM((species + 1, 8, LANES), f32),
            pltpu.VMEM((width * 8, LANES), f32),
            pltpu.VMEM((groups, FIRST, LANES), f32),
            pltpu.VMEM((groups, FIRST, LANES), f32),
            pltpu.VMEM((species, levels), f32),
        ],
        cost_estimate=pl.CostEstimate(
            flops=20_000_000_000, bytes_accessed=8_000_000, transcendentals=0
        ),
        compiler_params=pltpu.CompilerParams(vmem_limit_bytes=VMEM_LIMIT),
        name="first",
    )(
        pole,
        rate_index,
        tr,
        east_wind,
        north_wind,
        sunlit,
        from_west,
        from_east,
        coupling,
        rate_table,
        jnp.pad(kappa, (0, 1)).reshape(1, levels),
    )

    count = LIT_CAP - FIRST
    out = pl.pallas_call(
        functools.partial(second_kernel, *sizes),
        out_shape=shape((species * levels, lat_rows, lon_cols), bf16),
        in_specs=[smem] + [vmem] * 11,
        out_specs=vmem,
        scratch_shapes=[
            pltpu.VMEM((width, 2 * LANES), bf16),
            pltpu.VMEM((width, count), bf16),
            pltpu.VMEM((groups, count, LANES), f32),
            pltpu.VMEM((groups, count, LANES), f32),
            pltpu.VMEM((width * 8, LANES), f32),
        ],
        compiler_params=pltpu.CompilerParams(vmem_limit_bytes=VMEM_LIMIT),
        name="second",
    )(pole, part, top, bottom, from_south, from_north, xb, pick, fin, mix, tab, sunlit)
    return out.reshape(tracers.shape)


def solution(mesh):
    placed = (
        P(None, None, "lat", "lon"),
        P(None, "lat", "lon"),
        P(None, "lat", "lon"),
        P("lat", "lon"),
        P(),
        P(),
        P(),
        P(),
    )
    return jax.shard_map(
        local, mesh=mesh, in_specs=placed, out_specs=P(None, None, "lat", "lon"), check_vma=False
    )
```

time: 395 us -> 52.8 us (0.13)
  the two profiles are of different devices: /device:TPU:113 before, /device:TPU:143 now
where the time goes in v2:
time: 52.8 us; the launch traced here: 52.7 us
  Pallas kernels  39.7 us (75%)
  starting transfers between devices  12.7 us (24%)
    pallas_call x1, Pallas kernels, local(): pl.pallas_call(functools.partial(first_kernel, *sizes), out_shape=(shape(...  22.9 us
    pallas_call x1, Pallas kernels, local(): pl.pallas_call(functools.partial(second_kernel, *sizes), out_shape=shape(...  13.7 us
    ppermute x1, starting transfers between devices, local(): lax.ppermute(bottom, 'lat', [(i + 1, i) for i in range(nlat - 1)])  4.97 us
    ppermute x1, starting transfers between devices, local(): from_south = lax.ppermute(top, 'lat', [(i, i + 1) for i in range(nlat - 1)])  3.91 us
    ppermute x1, starting transfers between devices, local(): lax.ppermute(lon_pack, 'lon', [(i, (i + 1) % nlon) for i in range(nlon)])  3.18 us
    pallas_call x1, Pallas kernels, local(): pl.pallas_call(functools.partial(edge_kernel, *sizes), out_shape=(shape((...  3.05 us
  transfers between devices with their start and end apart: 4, of which 0 were waited for; matrix products, arithmetic and copies ran while one was open for 0% of the time, Pallas kernels for 44%

profile of v2, /device:TPU:143, one launch (start us, length us, event | category | flops | bytes accessed | tf_op | source)
XLA Modules:
  0.0 52.7 jit_solution(14434576629708910592)
XLA Ops:
  0.0 0.0 copy-start.4
  0.0 0.0 copy-start.3
  0.0 0.0 copy-start
  0.0 0.0 copy-start.9
  0.0 0.0 copy-start.5
  0.0 0.0 copy-start.8
  0.0 0.0 copy-start.7
  0.0 0.0 copy-start.6
  0.1 3.0 %edges.1 = (bf16[13,8,128]{2,1,0:T(8,128)(2,1)}, bf16[896,128]{1,0:T(8,128)(2,1)}, bf16[960,128]{1,0:T(8,128)(2,1)}) custom-call(bf16[768,8,128]{2,1,0:T(8,128)(2,1)} %bitcast.5, bf16[64,8,128]{2,1,0:T(8,128)(2,1)} %east.3, bf16[64,8,128]{2,1,0:T(8,128)(2,1)} %north.3), custom_call_target="tpu_custom_call" | custom-call | tf_op jit(solution)/shard_map/edges/pallas_call | solution.py:386
  3.1 0.7 %collective-permute-start.1 = (bf16[13,8,128]{2,1,0:T(8,128)(2,1)}, bf16[13,8,128]{2,1,0:T(8,128)(2,1)S(1)}, u32[]{:S(2)}, u32[]{:S(2)}) collective-permute-start(bf16[13,8,128]{2,1,0:T(8,128)(2,1)} %get-tuple-element.14), channel_id=1, source_target_pairs={{16,0},{32,16},{48,32},{64,48},{80,64},{96,80},{112,96},{128,112},... | collective-permute-start | bytes 79880 | tf_op jit(solution)/shard_map/ppermute | solution.py:403
  3.8 3.2 %collective-permute-start = (bf16[13,8,128]{2,1,0:T(8,128)(2,1)}, bf16[13,8,128]{2,1,0:T(8,128)(2,1)S(1)}, u32[]{:S(2)}, u32[]{:S(2)}) collective-permute-start(bf16[13,8,128]{2,1,0:T(8,128)(2,1)} %get-tuple-element.14), channel_id=1, source_target_pairs={{0,16},{16,32},{32,48},{48,64},{64,80},{80,96},{96,112},{112,128},... | collective-permute-start | bytes 79880 | tf_op jit(solution)/shard_map/ppermute | solution.py:402
  7.0 3.9 %collective-permute-start.2 = (bf16[896,128]{1,0:T(8,128)(2,1)}, bf16[896,128]{1,0:T(8,128)(2,1)S(1)}, u32[]{:S(2)}, u32[]{:S(2)}) collective-permute-start(bf16[896,128]{1,0:T(8,128)(2,1)} %get-tuple-element.16.top), channel_id=1, source_target_pairs={{0,1},{1,2},{2,3},{3,4},{4,5},{5,6},{6,7},{7,8},{8,9},{9,10},{10,1... | collective-permute-start | bytes 688136 | tf_op jit(solution)/shard_map/ppermute | solution.py:400
  10.9 5.0 %collective-permute-start.3 = (bf16[960,128]{1,0:T(8,128)(2,1)}, bf16[960,128]{1,0:T(8,128)(2,1)S(1)}, u32[]{:S(2)}, u32[]{:S(2)}) collective-permute-start(bf16[960,128]{1,0:T(8,128)(2,1)} %get-tuple-element.17.bottom), channel_id=1, source_target_pairs={{1,0},{2,1},{3,2},{4,3},{5,4},{6,5},{7,6},{8,7},{9,8},{10,9},{11,1... | collective-permute-start | bytes 737288 | tf_op jit(solution)/shard_map/ppermute | solution.py:401
  15.9 0.0 copy-done.9
  15.9 0.0 collective-permute-done.1.from_east
  15.9 0.0 collective-permute-done.from_west
  15.9 0.0 copy-done.4
  15.9 0.0 copy-done.3
  15.9 0.0 copy-done
  15.9 0.0 copy-done.5
  16.0 0.0 copy-done.8
  16.0 0.0 copy-done.7
  16.0 0.0 copy-done.6
  16.0 0.0 copy-start.1
  16.0 0.0 copy-start.2
  16.0 22.9 %first.1 = (f32[2,896,128]{2,1,0:T(8,128)S(1)}, bf16[896,1024]{1,0:T(8,128)(2,1)S(1)}, bf16[768,1024]{1,0:T(8,128)(2,1)S(1)}, bf16[896,512]{1,0:T(8,128)(2,1)S(1...) custom-call(s32[1]{0:T(128)} %bitcast.pole, s32[12]{0:T(128)S(1)} %copy-done.8, bf16[768,8,128]{2,1,0:T(8,128)(2,1)S(1)} %bitcast.6, ...), custom_call_target="tpu_custom_call" | custom-call | flops 20000000000 | bytes 8000000 | tf_op jit(solution)/shard_map/first/pallas_call | solution.py:406
  38.9 0.0 collective-permute-done.2.from_south
  38.9 0.0 collective-permute-done.3.from_north
  39.0 0.0 copy-done.1
  39.0 0.0 copy-done.2
  39.0 13.7 %second.1 = bf16[768,8,128]{2,1,0:T(8,128)(2,1)} custom-call(s32[1]{0:T(128)} %bitcast.pole, f32[2,896,128]{2,1,0:T(8,128)S(1)} %get-tuple-element.15.part, bf16[896,128]{1,0:T(8,128)(2,1)S(1)} %copy-done.2, bf16[960,128]{1,0:T(8,128)(2,1)S(1)} %copy-done.1, bf16[896,128]{1,0:T(8,128)(2,1)S(1)} %collective-permute-done.2.from_south, ...), custom_call_target="tpu_custom_call" | custom-call | tf_op jit(solution)/shard_map/second/pallas_call | solution.py:445
  (1 shorter events, 0.0 us)
Async XLA Ops:
  0.0 15.9 %copy-start.4 = (bf16[64,8,128]{2,1,0:T(8,128)(2,1)S(1)}, bf16[64,8,128]{2,1,0:T(8,128)(2,1)}, u32[]{:S(2)}) copy-start(bf16[64,8,128]{2,1,0:T(8,128)(2,1)} %north.3) | copy-start | bytes 393220
  0.0 15.9 %copy-start.3 = (bf16[64,8,128]{2,1,0:T(8,128)(2,1)S(1)}, bf16[64,8,128]{2,1,0:T(8,128)(2,1)}, u32[]{:S(2)}) copy-start(bf16[64,8,128]{2,1,0:T(8,128)(2,1)} %east.3) | copy-start | bytes 393220
  0.0 15.9 %copy-start = (bf16[12,64,8,128]{3,2,1,0:T(8,128)(2,1)S(1)}, bf16[12,64,8,128]{3,2,1,0:T(8,128)(2,1)}, u32[]{:S(2)}) copy-start(bf16[12,64,8,128]{3,2,1,0:T(8,128)(2,1)} %param.8) | copy-start | bytes 4718596
  0.0 15.9 %copy-start.9 = (f32[63]{0:T(128)S(1)}, f32[63]{0:T(128)}, u32[]{:S(2)}) copy-start(f32[63]{0:T(128)} %param.15) | copy-start | bytes 760
  0.0 15.9 %copy-start.5 = (s32[8,128]{1,0:T(8,128)S(1)}, s32[8,128]{1,0:T(8,128)}, u32[]{:S(2)}) copy-start(s32[8,128]{1,0:T(8,128)} %lit.3) | copy-start | bytes 12292
  0.0 15.9 %copy-start.8 = (s32[12]{0:T(128)S(1)}, s32[12]{0:T(128)}, u32[]{:S(2)}) copy-start(s32[12]{0:T(128)} %rate_index.1) | copy-start | bytes 148
  0.0 15.9 %copy-start.7 = (f32[8,64]{1,0:T(8,128)S(1)}, f32[8,64]{1,0:T(8,128)}, u32[]{:S(2)}) copy-start(f32[8,64]{1,0:T(8,128)} %rate_table.1) | copy-start | bytes 6148
  0.0 15.9 %copy-start.6 = (f32[12,12]{1,0:T(8,128)S(1)}, f32[12,12]{1,0:T(8,128)}, u32[]{:S(2)}) copy-start(f32[12,12]{1,0:T(8,128)} %coupling.1) | copy-start | bytes 1732
  3.1 12.8 %collective-permute-start.1 = (bf16[13,8,128]{2,1,0:T(8,128)(2,1)}, bf16[13,8,128]{2,1,0:T(8,128)(2,1)S(1)}, u32[]{:S(2)}, u32[]{:S(2)}) collective-permute-start(bf16[13,8,128]{2,1,0:T(8,128)(2,1)} %get-tuple-element.14), channel_id=1, source_target_pairs={{16,0},{32,16},{48,32},{64,48},{80,64},{96,80},{112,96},{128,112},... | collective-permute-start | bytes 79880 | tf_op jit(solution)/shard_map/ppermute | solution.py:403
  3.8 12.1 %collective-permute-start = (bf16[13,8,128]{2,1,0:T(8,128)(2,1)}, bf16[13,8,128]{2,1,0:T(8,128)(2,1)S(1)}, u32[]{:S(2)}, u32[]{:S(2)}) collective-permute-start(bf16[13,8,128]{2,1,0:T(8,128)(2,1)} %get-tuple-element.14), channel_id=1, source_target_pairs={{0,16},{16,32},{32,48},{48,64},{64,80},{80,96},{96,112},{112,128},... | collective-permute-start | bytes 79880 | tf_op jit(solution)/shard_map/ppermute | solution.py:402
  7.0 32.0 %collective-permute-start.2 = (bf16[896,128]{1,0:T(8,128)(2,1)}, bf16[896,128]{1,0:T(8,128)(2,1)S(1)}, u32[]{:S(2)}, u32[]{:S(2)}) collective-permute-start(bf16[896,128]{1,0:T(8,128)(2,1)} %get-tuple-element.16.top), channel_id=1, source_target_pairs={{0,1},{1,2},{2,3},{3,4},{4,5},{5,6},{6,7},{7,8},{8,9},{9,10},{10,1... | collective-permute-start | bytes 688136 | tf_op jit(solution)/shard_map/ppermute | solution.py:400
  10.9 28.1 %collective-permute-start.3 = (bf16[960,128]{1,0:T(8,128)(2,1)}, bf16[960,128]{1,0:T(8,128)(2,1)S(1)}, u32[]{:S(2)}, u32[]{:S(2)}) collective-permute-start(bf16[960,128]{1,0:T(8,128)(2,1)} %get-tuple-element.17.bottom), channel_id=1, source_target_pairs={{1,0},{2,1},{3,2},{4,3},{5,4},{6,5},{7,6},{8,7},{9,8},{10,9},{11,1... | collective-permute-start | bytes 737288 | tf_op jit(solution)/shard_map/ppermute | solution.py:401
  16.0 23.0 %copy-start.1 = (bf16[960,128]{1,0:T(8,128)(2,1)S(1)}, bf16[960,128]{1,0:T(8,128)(2,1)}, u32[]{:S(2)}) copy-start(bf16[960,128]{1,0:T(8,128)(2,1)} %get-tuple-element.17.bottom) | copy-start | bytes 737284
  16.0 23.0 %copy-start.2 = (bf16[896,128]{1,0:T(8,128)(2,1)S(1)}, bf16[896,128]{1,0:T(8,128)(2,1)}, u32[]{:S(2)}) copy-start(bf16[896,128]{1,0:T(8,128)(2,1)} %get-tuple-element.16.top) | copy-start | bytes 688132

commit v3 on v2

--- a/solution.py
+++ b/solution.py
@@ -11,7 +11,9 @@
 LANES = 128
 LIT_CAP = 768
 FIRST = 512
-CHUNK = 64
+CHUNK_FIRST = 256
+CHUNK_SECOND = 128
+UNROLL = 3
 VMEM_LIMIT = 24 << 20
 NT = (((1,), (1,)), ((), ()))
 f32, bf16 = jnp.float32, jnp.bfloat16
@@ -25,13 +27,29 @@
     return (k % groups) * LANES + (k // groups) * species + s
 
 
-def edge_kernel(species, levels, groups, tr, east, north, lon_out, top_out, bottom_out, rows, vrow):
+def edge_kernel(
+    species,
+    levels,
+    groups,
+    tr,
+    east,
+    north,
+    lon_out,
+    lat_a,
+    lat_b,
+    top_out,
+    wind_out,
+    rows,
+    vrow,
+):
     lane = iota((8, LANES), 1)
     zero = jnp.zeros((8, LANES), f32)
     for r in range(groups):
         for p in range(LANES):
             if p >= (LANES // species) * species or (p // species) * groups + r >= levels:
                 rows[pl.ds((r * LANES + p) * 8, 8), :] = zero
+    for k in range(levels):
+        vrow[pl.ds(k * 8, 8), :] = north[k].astype(f32)
     for s in range(species + 1):
         packed = zero
         for k in range(levels):
@@ -40,36 +58,40 @@
                 rows[pl.ds(place(k, s, species, groups) * 8, 8), :] = cell
             else:
                 cell = east[k].astype(f32)
-                vrow[pl.ds(k * 8, 8), :] = north[k].astype(f32)
             here = (lane == 2 * k) | (lane == (2 * k - 1) % LANES)
             moved = pltpu.roll(cell, 2 * k, 1) if k else cell
             packed = jnp.where(here, moved, packed)
         lon_out[s] = packed.astype(bf16)
     width = groups * LANES
-    bottom_out[:width] = rows[pl.ds(0, width, stride=8), :].astype(bf16)
-    bottom_out[width:] = vrow[pl.ds(0, levels, stride=8), :].astype(bf16)
-    top_out[...] = rows[pl.ds(7, width, stride=8), :].astype(bf16)
-
-
-def run_chemistry(groups, species, count, mix, loss, kappa, state, made, emit):
+    is_odd = lax.axis_index("lat") % 2 > 0
+    bottom = rows[pl.ds(0, width, stride=8), :]
+    top = rows[pl.ds(7, width, stride=8), :]
+    wind = vrow[pl.ds(0, levels, stride=8), :].astype(bf16)
+    lat_a[:width] = jnp.where(is_odd, bottom, top).astype(bf16)
+    lat_b[:width] = jnp.where(is_odd, top, bottom).astype(bf16)
+    lat_a[width:] = wind
+    lat_b[width:] = wind
+    wind_out[...] = wind
+    top_out[...] = top.astype(bf16)
+
+
+def run_chemistry(groups, species, count, size, mix, tab, state, made, emit):
+    kappa = tab.at[8:16]
+
     def produce(parts, i):
-        stack = []
-        for q in parts:
+        for r, q in enumerate(parts):
             high = q.astype(bf16)
             low = (q - high.astype(f32)).astype(bf16)
-            stack.append(jnp.concatenate([high, low], axis=1))
-        res = jnp.dot(jnp.concatenate(stack, axis=0), mix[...], preferred_element_type=f32)
-        for r in range(groups):
-            part = res[r * CHUNK : (r + 1) * CHUNK]
-            made[r, i * CHUNK : (i + 1) * CHUNK, :] = part[:, :LANES] + part[:, LANES:]
+            pair = jnp.concatenate([high, low], axis=1)
+            res = jnp.dot(pair, mix[r], preferred_element_type=f32)
+            made[r, i * size : (i + 1) * size, :] = res[:, :LANES] + res[:, LANES:]
 
     def react(i):
-        at = slice(i * CHUNK, (i + 1) * CHUNK)
+        at = slice(i * size, (i + 1) * size)
         y = []
         for r in range(groups):
             q = state[r, at, :]
-            lo = loss[r : r + 1, :]
-            y.append(made[r, at, :] / ((1.0 + lo) + lo * (q * q)))
+            y.append(made[r, at, :] / (tab[r : r + 1, :] + q * q))
         flux = []
         for r in range(groups):
             if r + 1 < groups:
@@ -85,43 +107,41 @@
             res.append(q)
         return res
 
-    chunks = count // CHUNK
+    chunks = count // size
     for i in range(chunks):
-        produce([state[r, i * CHUNK : (i + 1) * CHUNK, :] for r in range(groups)], i)
+        produce([state[r, i * size : (i + 1) * size, :] for r in range(groups)], i)
 
     def substep(step, carry):
-        for i in range(chunks):
-            produce(react(i), i)
+        for _ in range(UNROLL):
+            for i in range(chunks):
+                produce(react(i), i)
         return carry
 
-    lax.fori_loop(0, SUBSTEPS - 1, substep, 0)
+    lax.fori_loop(0, (SUBSTEPS - 1) // UNROLL, substep, 0)
     for i in range(chunks):
         react(i)
     for r in range(groups):
         emit(r, state[r, :count, :].T.astype(bf16))
 
 
-def tables(species, levels, groups, coupling, rate_table, rate_index, kappa, mix, tab, loss_rows):
-    slots = LANES // species
+def tables(species, levels, groups, small, rate_index, mix, tab, loss_rows):
+    slots, rates = LANES // species, small.shape[0] - 1
     for s in range(species):
-        loss_rows[s : s + 1, :] = rate_table[pl.ds(rate_index[s], 1), :]
+        loss_rows[s : s + 1, :] = small[pl.ds(species + rate_index[s], 1), :]
     p = iota((LANES, species), 0)
     slot = (p * 171) >> 11
     spread = jnp.logical_and(p - slot * species == iota((LANES, species), 1), slot < slots)
     spread = spread.astype(f32)
-    full = coupling[...] + (iota((species, species), 0) == iota((species, species), 1)).astype(f32)
+    full = small[:species, :species] + (iota((species, species), 0) == iota((species, species), 1)).astype(f32)
     same = ((iota((LANES, LANES), 0) * 171) >> 11) == ((iota((LANES, LANES), 1) * 171) >> 11)
 
     def block(part):
         half = lax.dot_general(spread, part.astype(f32), NT, preferred_element_type=f32)
         wide = lax.dot_general(half, spread, NT, preferred_element_type=f32)
-        return jnp.where(same, wide, 0.0).astype(bf16)
+        return jnp.where(same, wide, 0.0)
 
     high = full.astype(bf16)
-    low = (full - high.astype(f32)).astype(bf16)
-    for at in (0, LANES):
-        mix[at : at + LANES, :LANES] = block(high)
-        mix[at : at + LANES, LANES:] = block(low)
+    whole = block(high) + block((full - high.astype(f32)).astype(bf16))
     width = groups * LANES
     col = iota((levels, width), 1)
     lane = col & (LANES - 1)
@@ -133,27 +153,32 @@
     col = iota((species, width), 1) & (LANES - 1)
     mine = col - ((col * 171) >> 11) * species == iota((species, width), 0)
     loss = jnp.sum(jnp.where(mine, spread_loss, 0.0), axis=0, keepdims=True)
-    kap = jnp.dot(kappa[...], sel, preferred_element_type=f32, precision=exact)
+    kap = jnp.dot(small[rates:, :], sel, preferred_element_type=f32, precision=exact)
+    inverse = jnp.where(loss > 0.0, 1.0 / jnp.where(loss > 0.0, loss, 1.0), 0.0)
     for r in range(groups):
-        tab[r : r + 1, :] = loss[:, r * LANES : (r + 1) * LANES]
+        mine = inverse[:, r * LANES : (r + 1) * LANES]
+        tab[r : r + 1, :] = 1.0 + mine
         tab[8 + r : 9 + r, :] = kap[:, r * LANES : (r + 1) * LANES]
+        scaled = whole * mine
+        high = scaled.astype(bf16)
+        low = (scaled - high.astype(f32)).astype(bf16)
+        for at in (0, LANES):
+            mix[r, at : at + LANES, :LANES] = high
+            mix[r, at : at + LANES, LANES:] = low
 
 
 def first_kernel(
     species,
     levels,
     groups,
-    pole,
     rate_index,
     tr,
     east,
     north,
     lit,
-    from_west,
-    from_east,
-    coupling,
-    rate_table,
-    kappa,
+    lon_a,
+    lon_b,
+    small,
     part_out,
     xb,
     pick,
@@ -171,12 +196,14 @@
     width = groups * LANES
     slots = LANES // species
 
-    tables(species, levels, groups, coupling, rate_table, rate_index, kappa, mix, tab, loss_rows)
+    tables(species, levels, groups, small, rate_index, mix, tab, loss_rows)
+    is_odd = lax.axis_index("lon") % 2 > 0
     for s in range(species + 1):
-        lon_edge[s] = jnp.where(
-            lane % 2 == 0, from_east[s].astype(f32), pltpu.roll(from_west[s].astype(f32), 2, 1)
-        )
-    at_pole = pole[0] > 0
+        got_a, got_b = lon_a[s].astype(f32), lon_b[s].astype(f32)
+        from_east = jnp.where(is_odd, got_b, got_a)
+        from_west = jnp.where(is_odd, got_a, got_b)
+        lon_edge[s] = jnp.where(lane % 2 == 0, from_east, pltpu.roll(from_west, 2, 1))
+    at_pole = lax.axis_index("lat") == 0
 
     zero_tile = jnp.zeros((8, LANES), f32)
     for r in range(groups):
@@ -277,19 +304,18 @@
     def emit(r, value):
         fin[r * LANES : (r + 1) * LANES, :] = value
 
-    run_chemistry(groups, species, FIRST, mix, tab, tab.at[8:16], state, made, emit)
+    run_chemistry(groups, species, FIRST, CHUNK_FIRST, mix, tab, state, made, emit)
 
 
 def second_kernel(
     species,
     levels,
     groups,
-    pole,
     part,
     top,
-    bottom,
-    from_south,
-    from_north,
+    wind,
+    lat_a,
+    lat_b,
     xb,
     pick,
     fin,
@@ -310,14 +336,18 @@
     slot = ((row & (LANES - 1)) * 171) >> 11
     sel = jnp.logical_and(iota((width, levels), 1) == slot * groups + (row >> 7), slot < slots)
     sel = sel.astype(f32).astype(bf16)
-    v_here = jnp.dot(sel, bottom[width:, :], preferred_element_type=f32)
-    v_here = jnp.where(pole[0] > 0, 0.0, jnp.maximum(v_here, 0.0))
-    xe[:, :LANES] = (part[0] + v_here * from_south[...].astype(f32)).astype(bf16)
-    v_next = jnp.dot(sel, from_north[width:, :], preferred_element_type=f32)
+    is_odd = lax.axis_index("lat") % 2 > 0
+    got_a, got_b = lat_a[:width].astype(f32), lat_b[:width].astype(f32)
+    south = jnp.where(is_odd, got_a, got_b)
+    north = jnp.where(is_odd, got_b, got_a)
+    v_here = jnp.dot(sel, wind[...], preferred_element_type=f32)
+    v_here = jnp.where(lax.axis_index("lat") == 0, 0.0, jnp.maximum(v_here, 0.0))
+    xe[:, :LANES] = (part[0] + v_here * south).astype(bf16)
+    wind_a, wind_b = lat_a[width:].astype(f32), lat_b[width:].astype(f32)
+    v_next = jnp.where(is_odd, wind_b, wind_a).astype(bf16)
+    v_next = jnp.dot(sel, v_next, preferred_element_type=f32)
     xe[:, LANES:] = (
-        part[1]
-        - jnp.maximum(v_next, 0.0) * top[...].astype(f32)
-        - jnp.minimum(v_next, 0.0) * from_north[:width, :].astype(f32)
+        part[1] - jnp.maximum(v_next, 0.0) * top[...].astype(f32) - jnp.minimum(v_next, 0.0) * north
     ).astype(bf16)
 
     rest = slice(FIRST, LIT_CAP)
@@ -338,7 +368,7 @@
     def emit(r, value):
         fin_b[r * LANES : (r + 1) * LANES, :] = value
 
-    run_chemistry(groups, species, LIT_CAP - FIRST, mix, tab, tab.at[8:16], state, made, emit)
+    run_chemistry(groups, species, LIT_CAP - FIRST, CHUNK_SECOND, mix, tab, state, made, emit)
 
     def settle(j, got, moved):
         keep = lit_mask[j : j + 1, :]
@@ -383,26 +413,37 @@
     vmem = pl.BlockSpec(memory_space=pltpu.VMEM)
     smem = pl.BlockSpec(memory_space=pltpu.SMEM)
     shape = jax.ShapeDtypeStruct
-    lon_pack, top, bottom = pl.pallas_call(
+    lon_pack, send_a, send_b, top, wind = pl.pallas_call(
         functools.partial(edge_kernel, *sizes),
         out_shape=(
             shape((species + 1, 8, LANES), bf16),
+            shape((width + levels, LANES), bf16),
+            shape((width + levels, LANES), bf16),
             shape((width, LANES), bf16),
-            shape((width + levels, LANES), bf16),
+            shape((levels, LANES), bf16),
         ),
         in_specs=[vmem] * 3,
-        out_specs=(vmem,) * 3,
-        scratch_shapes=[pltpu.VMEM((width * 8, LANES), f32), pltpu.VMEM((levels * 8, LANES), f32)],
+        out_specs=(vmem,) * 5,
+        scratch_shapes=[
+            pltpu.VMEM((width * 8, LANES), f32),
+            pltpu.VMEM((levels * 8, LANES), f32),
+        ],
         name="edges",
     )(tr, east_wind, north_wind)
 
     nlon, nlat = lax.axis_size("lon"), lax.axis_size("lat")
-    from_south = lax.ppermute(top, "lat", [(i, i + 1) for i in range(nlat - 1)])
-    from_north = lax.ppermute(bottom, "lat", [(i + 1, i) for i in range(nlat - 1)])
-    from_west = lax.ppermute(lon_pack, "lon", [(i, (i + 1) % nlon) for i in range(nlon)])
-    from_east = lax.ppermute(lon_pack, "lon", [((i + 1) % nlon, i) for i in range(nlon)])
-    pole = (lax.axis_index("lat") == 0).astype(jnp.int32).reshape(1)
-
+    pairs = [(i, i ^ 1) for i in range(nlon)]
+    others = [(i, (i + 1) % nlon if i % 2 else (i - 1) % nlon) for i in range(nlon)]
+    lon_a = lax.ppermute(lon_pack, "lon", pairs)
+    lon_b = lax.ppermute(lon_pack, "lon", others)
+    pairs = [(i, i ^ 1) for i in range(nlat)]
+    others = [(i, i + 1 if i % 2 else i - 1) for i in range(1, nlat - 1)]
+    lat_a = lax.ppermute(send_a, "lat", pairs)
+    lat_b = lax.ppermute(send_b, "lat", others) if others else jnp.zeros_like(send_b)
+
+    small = jnp.concatenate(
+        [jnp.pad(coupling, ((0, 0), (0, levels - species))), rate_table, jnp.pad(kappa, (0, 1))[None]]
+    )
     part, xb, pick, fin, mix, tab = pl.pallas_call(
         functools.partial(first_kernel, *sizes),
         out_shape=(
@@ -410,10 +451,10 @@
             shape((width, 8 * LANES), bf16),
             shape((LIT_CAP, 8 * LANES), bf16),
             shape((width, FIRST), bf16),
-            shape((2 * LANES, 2 * LANES), bf16),
+            shape((groups, 2 * LANES, 2 * LANES), bf16),
             shape((16, LANES), f32),
         ),
-        in_specs=[smem] * 2 + [vmem] * 9,
+        in_specs=[smem] + [vmem] * 7,
         out_specs=(vmem,) * 6,
         scratch_shapes=[
             pltpu.VMEM((species + 1, 8, LANES), f32),
@@ -428,24 +469,21 @@
         compiler_params=pltpu.CompilerParams(vmem_limit_bytes=VMEM_LIMIT),
         name="first",
     )(
-        pole,
         rate_index,
         tr,
         east_wind,
         north_wind,
         sunlit,
-        from_west,
-        from_east,
-        coupling,
-        rate_table,
-        jnp.pad(kappa, (0, 1)).reshape(1, levels),
+        lon_a,
+        lon_b,
+        small,
     )
 
     count = LIT_CAP - FIRST
     out = pl.pallas_call(
         functools.partial(second_kernel, *sizes),
         out_shape=shape((species * levels, lat_rows, lon_cols), bf16),
-        in_specs=[smem] + [vmem] * 11,
+        in_specs=[vmem] * 11,
         out_specs=vmem,
         scratch_shapes=[
             pltpu.VMEM((width, 2 * LANES), bf16),
@@ -456,7 +494,7 @@
         ],
         compiler_params=pltpu.CompilerParams(vmem_limit_bytes=VMEM_LIMIT),
         name="second",
-    )(pole, part, top, bottom, from_south, from_north, xb, pick, fin, mix, tab, sunlit)
+    )(part, top, wind, lat_a, lat_b, xb, pick, fin, mix, tab, sunlit)
     return out.reshape(tracers.shape)
 
 

time: 52.8 us -> 48.8 us (0.924)
  the two profiles are of different devices: /device:TPU:143 before, /device:TPU:113 now
where the time goes in v3:
time: 48.8 us; the launch traced here: 48.6 us
  Pallas kernels  36.5 us (75%)
  starting transfers between devices  11.2 us (23%)
  other arithmetic  0.7 us (1%)
    pallas_call x1, Pallas kernels, local(): pl.pallas_call(functools.partial(first_kernel, *sizes), out_shape=(shape(...  20.9 us
    pallas_call x1, Pallas kernels, local(): pl.pallas_call(functools.partial(second_kernel, *sizes), out_shape=shape(...  12.5 us
    ppermute x1, starting transfers between devices, local(): lax.ppermute(send_b, 'lat', others)  7.26 us
    pallas_call x1, Pallas kernels, local(): pl.pallas_call(functools.partial(edge_kernel, *sizes), out_shape=(shape((...  3.15 us
    ppermute x1, starting transfers between devices, local(): lon_a = lax.ppermute(lon_pack, 'lon', pairs)  1.82 us
    ppermute x1, starting transfers between devices, local(): lon_b = lax.ppermute(lon_pack, 'lon', others)  1.77 us
  transfers between devices with their start and end apart: 4, of which 0 were waited for; matrix products, arithmetic and copies ran while one was open for 1% of the time, Pallas kernels for 43%

profile of v3, /device:TPU:113, one launch (start us, length us, event | category | flops | bytes accessed | tf_op | source)
XLA Modules:
  0.0 48.6 jit_solution(14110646954744011625)
XLA Ops:
  0.0 0.0 copy-start.3
  0.0 0.0 copy-start.2
  0.0 0.0 copy-start
  0.0 0.0 copy-start.8
  0.0 0.0 copy-start.7
  0.0 0.0 copy-start.5
  0.0 0.0 copy-start.6
  0.0 3.2 %edges.1 = (bf16[13,8,128]{2,1,0:T(8,128)(2,1)}, bf16[960,128]{1,0:T(8,128)(2,1)}, bf16[960,128]{1,0:T(8,128)(2,1)}, bf16[896,128]{1,0:T(8,128)(2,1)}, bf16[64,128]{1,0:T(8,128)(2,1)}) custom-call(bf16[768,8,128]{2,1,0:T(8,128)(2,1)} %bitcast.4, bf16[64,8,128]{2,1,0:T(8,128)(2,1)} %east.3, bf16[64,8,128]{2,1,0:T(8,128)(2,1)} %north.3), custom_call_target="tpu_custom_call" | custom-call | tf_op jit(solution)/shard_map/edges/pallas_call | solution.py:416
  3.2 1.8 %collective-permute-start.1 = (bf16[13,8,128]{2,1,0:T(8,128)(2,1)}, bf16[13,8,128]{2,1,0:T(8,128)(2,1)S(1)}, u32[]{:S(2)}, u32[]{:S(2)}) collective-permute-start(bf16[13,8,128]{2,1,0:T(8,128)(2,1)} %get-tuple-element.16), channel_id=1, source_target_pairs={{0,240},{16,32},{32,16},{48,64},{64,48},{80,96},{96,80},{112,128},... | collective-permute-start | bytes 79880 | tf_op jit(solution)/shard_map/ppermute | solution.py:438
  5.0 1.8 %collective-permute-start = (bf16[13,8,128]{2,1,0:T(8,128)(2,1)}, bf16[13,8,128]{2,1,0:T(8,128)(2,1)S(1)}, u32[]{:S(2)}, u32[]{:S(2)}) collective-permute-start(bf16[13,8,128]{2,1,0:T(8,128)(2,1)} %get-tuple-element.16), channel_id=1, source_target_pairs={{0,16},{16,0},{32,48},{48,32},{64,80},{80,64},{96,112},{112,96},{1... | collective-permute-start | bytes 79880 | tf_op jit(solution)/shard_map/ppermute | solution.py:437
  6.8 0.3 collective-permute-start.2
  7.1 7.3 %collective-permute-start.3 = (bf16[960,128]{1,0:T(8,128)(2,1)}, bf16[960,128]{1,0:T(8,128)(2,1)S(1)}, u32[]{:S(2)}, u32[]{:S(2)}) collective-permute-start(bf16[960,128]{1,0:T(8,128)(2,1)} %get-tuple-element.21), channel_id=1, source_target_pairs={{1,2},{2,1},{3,4},{4,3},{5,6},{6,5},{7,8},{8,7},{9,10},{10,9},{11,... | collective-permute-start | bytes 737288 | tf_op jit(solution)/shard_map/ppermute | solution.py:442
  14.4 0.0 copy-done.8
  14.4 0.0 copy-done.7
  14.4 0.7 %fusion.small = f32[21,64]{1,0:T(8,128)S(1)} fusion(f32[12,12]{1,0:T(8,128)S(1)} %copy-done.7, f32[1,64]{1,0:T(1,128)S(1)} %pad_bitcast_fusion, f32[8,64]{1,0:T(8,128)} %param.13), kind=kLoop, calls=%fused_computation.1 | loop fusion | flops 5376 | bytes 8256 | tf_op jit(solution)/shard_map/concatenate | solution.py:444
  15.1 0.0 copy-start.1
  15.1 0.0 copy-start.4
  15.2 0.0 collective-permute-done.1.lon_b
  15.2 0.0 collective-permute-done.lon_a
  15.2 0.0 copy-done.3
  15.2 0.0 copy-done.2
  15.2 0.0 copy-done
  15.2 0.0 copy-done.5
  15.2 0.0 copy-done.6
  15.2 20.9 %first.1 = (f32[2,896,128]{2,1,0:T(8,128)S(1)}, bf16[896,1024]{1,0:T(8,128)(2,1)S(1)}, bf16[768,1024]{1,0:T(8,128)(2,1)S(1)}, bf16[896,512]{1,0:T(8,128)(2,1)S(1...) custom-call(s32[12]{0:T(128)S(1)} %copy-done.6, bf16[768,8,128]{2,1,0:T(8,128)(2,1)S(1)} %bitcast.5, ...), custom_call_target="tpu_custom_call" | custom-call | flops 20000000000 | bytes 8000000 | tf_op jit(solution)/shard_map/first/pallas_call | solution.py:447
  36.1 0.0 collective-permute-done.2.lat_a
  36.1 0.0 collective-permute-done.3.lat_b
  36.1 0.0 copy-done.1
  36.2 0.0 copy-done.4
  36.2 12.5 %second.1 = bf16[768,8,128]{2,1,0:T(8,128)(2,1)} custom-call(f32[2,896,128]{2,1,0:T(8,128)S(1)} %get-tuple-element.17.part, bf16[896,128]{1,0:T(8,128)(2,1)S(1)} %copy-done.1, bf16[64,128]{1,0:T(8,128)(2,1)S(1)} %copy-done.4, bf16[960,128]{1,0:T(8,128)(2,1)S(1)} %collective-permute-done.2.lat_a, bf16[960,128]{1,0:T(8,128)(2,1)S(1)} %collective-permute-done.3.lat_b, ...), custom_call_target="tpu_custom_call" | custom-call | tf_op jit(solution)/shard_map/second/pallas_call | solution.py:483
  (1 shorter events, 0.0 us)
Async XLA Ops:
  0.0 15.2 %copy-start.3 = (bf16[64,8,128]{2,1,0:T(8,128)(2,1)S(1)}, bf16[64,8,128]{2,1,0:T(8,128)(2,1)}, u32[]{:S(2)}) copy-start(bf16[64,8,128]{2,1,0:T(8,128)(2,1)} %north.3) | copy-start | bytes 393220
  0.0 15.2 %copy-start.2 = (bf16[64,8,128]{2,1,0:T(8,128)(2,1)S(1)}, bf16[64,8,128]{2,1,0:T(8,128)(2,1)}, u32[]{:S(2)}) copy-start(bf16[64,8,128]{2,1,0:T(8,128)(2,1)} %east.3) | copy-start | bytes 393220
  0.0 15.2 %copy-start = (bf16[12,64,8,128]{3,2,1,0:T(8,128)(2,1)S(1)}, bf16[12,64,8,128]{3,2,1,0:T(8,128)(2,1)}, u32[]{:S(2)}) copy-start(bf16[12,64,8,128]{3,2,1,0:T(8,128)(2,1)} %param.8) | copy-start | bytes 4718596
  0.0 14.4 %copy-start.8 = (f32[63]{0:T(128)S(1)}, f32[63]{0:T(128)}, u32[]{:S(2)}) copy-start(f32[63]{0:T(128)} %param.15) | copy-start | bytes 760
  0.0 14.4 %copy-start.7 = (f32[12,12]{1,0:T(8,128)S(1)}, f32[12,12]{1,0:T(8,128)}, u32[]{:S(2)}) copy-start(f32[12,12]{1,0:T(8,128)} %param.12) | copy-start | bytes 1732
  0.0 15.2 %copy-start.5 = (s32[8,128]{1,0:T(8,128)S(1)}, s32[8,128]{1,0:T(8,128)}, u32[]{:S(2)}) copy-start(s32[8,128]{1,0:T(8,128)} %lit.3) | copy-start | bytes 12292
  0.0 15.2 %copy-start.6 = (s32[12]{0:T(128)S(1)}, s32[12]{0:T(128)}, u32[]{:S(2)}) copy-start(s32[12]{0:T(128)} %rate_index.1) | copy-start | bytes 148
  3.2 12.0 %collective-permute-start.1 = (bf16[13,8,128]{2,1,0:T(8,128)(2,1)}, bf16[13,8,128]{2,1,0:T(8,128)(2,1)S(1)}, u32[]{:S(2)}, u32[]{:S(2)}) collective-permute-start(bf16[13,8,128]{2,1,0:T(8,128)(2,1)} %get-tuple-element.16), channel_id=1, source_target_pairs={{0,240},{16,32},{32,16},{48,64},{64,48},{80,96},{96,80},{112,128},... | collective-permute-start | bytes 79880 | tf_op jit(solution)/shard_map/ppermute | solution.py:438
  5.0 10.2 %collective-permute-start = (bf16[13,8,128]{2,1,0:T(8,128)(2,1)}, bf16[13,8,128]{2,1,0:T(8,128)(2,1)S(1)}, u32[]{:S(2)}, u32[]{:S(2)}) collective-permute-start(bf16[13,8,128]{2,1,0:T(8,128)(2,1)} %get-tuple-element.16), channel_id=1, source_target_pairs={{0,16},{16,0},{32,48},{48,32},{64,80},{80,64},{96,112},{112,96},{1... | collective-permute-start | bytes 79880 | tf_op jit(solution)/shard_map/ppermute | solution.py:437
  6.8 29.3 %collective-permute-start.2 = (bf16[960,128]{1,0:T(8,128)(2,1)}, bf16[960,128]{1,0:T(8,128)(2,1)S(1)}, u32[]{:S(2)}, u32[]{:S(2)}) collective-permute-start(bf16[960,128]{1,0:T(8,128)(2,1)} %get-tuple-element.20), channel_id=1, source_target_pairs={{0,1},{1,0},{2,3},{3,2},{4,5},{5,4},{6,7},{7,6},{8,9},{9,8},{10,11... | collective-permute-start | bytes 737288 | tf_op jit(solution)/shard_map/ppermute | solution.py:441
  7.1 29.0 %collective-permute-start.3 = (bf16[960,128]{1,0:T(8,128)(2,1)}, bf16[960,128]{1,0:T(8,128)(2,1)S(1)}, u32[]{:S(2)}, u32[]{:S(2)}) collective-permute-start(bf16[960,128]{1,0:T(8,128)(2,1)} %get-tuple-element.21), channel_id=1, source_target_pairs={{1,2},{2,1},{3,4},{4,3},{5,6},{6,5},{7,8},{8,7},{9,10},{10,9},{11,... | collective-permute-start | bytes 737288 | tf_op jit(solution)/shard_map/ppermute | solution.py:442
  15.1 21.0 %copy-start.1 = (bf16[896,128]{1,0:T(8,128)(2,1)S(1)}, bf16[896,128]{1,0:T(8,128)(2,1)}, u32[]{:S(2)}) copy-start(bf16[896,128]{1,0:T(8,128)(2,1)} %get-tuple-element.18.top) | copy-start | bytes 688132
  15.1 21.0 %copy-start.4 = (bf16[64,128]{1,0:T(8,128)(2,1)S(1)}, bf16[64,128]{1,0:T(8,128)(2,1)}, u32[]{:S(2)}) copy-start(bf16[64,128]{1,0:T(8,128)(2,1)} %get-tuple-element.19.wind) | copy-start | bytes 49156

commit v4 on v3

--- a/solution.py
+++ b/solution.py
@@ -13,7 +13,8 @@
 FIRST = 512
 CHUNK_FIRST = 256
 CHUNK_SECOND = 128
-UNROLL = 3
+UNROLL = 5
+BLOCKS = (1, 2, 3, 4, 5, 6, 0, 7)
 VMEM_LIMIT = 24 << 20
 NT = (((1,), (1,)), ((), ()))
 f32, bf16 = jnp.float32, jnp.bfloat16
@@ -75,7 +76,7 @@
     top_out[...] = top.astype(bf16)
 
 
-def run_chemistry(groups, species, count, size, mix, tab, state, made, emit):
+def run_chemistry(groups, species, count, size, mix, tab, state, made, emit, beside=None):
     kappa = tab.at[8:16]
 
     def produce(parts, i):
@@ -112,6 +113,8 @@
         produce([state[r, i * size : (i + 1) * size, :] for r in range(groups)], i)
 
     def substep(step, carry):
+        if beside is not None:
+            beside(step)
         for _ in range(UNROLL):
             for i in range(chunks):
                 produce(react(i), i)
@@ -124,15 +127,15 @@
         emit(r, state[r, :count, :].T.astype(bf16))
 
 
-def tables(species, levels, groups, small, rate_index, mix, tab, loss_rows):
-    slots, rates = LANES // species, small.shape[0] - 1
+def tables(species, levels, groups, coupling, rate_table, kappa, rate_index, mix, tab, loss_rows):
+    slots = LANES // species
     for s in range(species):
-        loss_rows[s : s + 1, :] = small[pl.ds(species + rate_index[s], 1), :]
+        loss_rows[s : s + 1, :] = rate_table[pl.ds(rate_index[s], 1), :]
     p = iota((LANES, species), 0)
     slot = (p * 171) >> 11
     spread = jnp.logical_and(p - slot * species == iota((LANES, species), 1), slot < slots)
     spread = spread.astype(f32)
-    full = small[:species, :species] + (iota((species, species), 0) == iota((species, species), 1)).astype(f32)
+    full = coupling[...] + (iota((species, species), 0) == iota((species, species), 1)).astype(f32)
     same = ((iota((LANES, LANES), 0) * 171) >> 11) == ((iota((LANES, LANES), 1) * 171) >> 11)
 
     def block(part):
@@ -153,7 +156,7 @@
     col = iota((species, width), 1) & (LANES - 1)
     mine = col - ((col * 171) >> 11) * species == iota((species, width), 0)
     loss = jnp.sum(jnp.where(mine, spread_loss, 0.0), axis=0, keepdims=True)
-    kap = jnp.dot(small[rates:, :], sel, preferred_element_type=f32, precision=exact)
+    kap = jnp.dot(kappa[...], sel[: levels - 1], preferred_element_type=f32, precision=exact)
     inverse = jnp.where(loss > 0.0, 1.0 / jnp.where(loss > 0.0, loss, 1.0), 0.0)
     for r in range(groups):
         mine = inverse[:, r * LANES : (r + 1) * LANES]
@@ -178,7 +181,9 @@
     lit,
     lon_a,
     lon_b,
-    small,
+    coupling,
+    rate_table,
+    kappa,
     part_out,
     xb,
     pick,
@@ -196,7 +201,9 @@
     width = groups * LANES
     slots = LANES // species
 
-    tables(species, levels, groups, small, rate_index, mix, tab, loss_rows)
+    tables(
+        species, levels, groups, coupling, rate_table, kappa, rate_index, mix, tab, loss_rows
+    )
     is_odd = lax.axis_index("lon") % 2 > 0
     for s in range(species + 1):
         got_a, got_b = lon_a[s].astype(f32), lon_b[s].astype(f32)
@@ -278,23 +285,22 @@
     slot = jnp.where(lit_mask, slot, -1.0).astype(jnp.int32)
 
     order = iota((LIT_CAP, LANES), 0)
-    for j in range(8):
-        pick[:, j * LANES : (j + 1) * LANES] = (
+    for i, j in enumerate(BLOCKS):
+        pick[:, i * LANES : (i + 1) * LANES] = (
             (order == slot[j : j + 1, :]).astype(f32).astype(bf16)
         )
         rows = adv[pl.ds(j, width, stride=8), :]
-        if 0 < j < 7:
-            xb[:, j * LANES : (j + 1) * LANES] = rows.astype(bf16)
+        if i < 6:
+            xb[:, i * LANES : (i + 1) * LANES] = rows.astype(bf16)
         else:
-            xb[:, j * LANES : (j + 1) * LANES] = jnp.zeros((width, LANES), bf16)
-            part_out[j // 7] = rows
-
-    span = slice(LANES, 7 * LANES)
+            part_out[i - 6] = rows
+
+    span = slice(0, 6 * LANES)
     for r in range(0, groups, 2):
         n = min(2, groups - r)
         got = lax.dot_general(
             pick[:FIRST, span],
-            xb[r * LANES : (r + n) * LANES, span],
+            xb[r * LANES : (r + n) * LANES, :],
             NT,
             preferred_element_type=f32,
         )
@@ -328,6 +334,8 @@
     state,
     made,
     back,
+    done,
+    sent,
 ):
     width = groups * LANES
     slots = LANES // species
@@ -351,16 +359,14 @@
     ).astype(bf16)
 
     rest = slice(FIRST, LIT_CAP)
-    span = slice(LANES, 7 * LANES)
     for r in range(0, groups, 2):
         n = min(2, groups - r)
         rows = slice(r * LANES, (r + n) * LANES)
-        got = lax.dot_general(pick[rest, span], xb[rows, span], NT, preferred_element_type=f32)
-        got = got + lax.dot_general(
-            pick[rest, :LANES], xe[rows, :LANES], NT, preferred_element_type=f32
+        got = lax.dot_general(
+            pick[rest, : 6 * LANES], xb[rows, :], NT, preferred_element_type=f32
         )
         got = got + lax.dot_general(
-            pick[rest, 7 * LANES :], xe[rows, LANES:], NT, preferred_element_type=f32
+            pick[rest, 6 * LANES :], xe[rows, :], NT, preferred_element_type=f32
         )
         for i in range(n):
             state[r + i] = got[:, i * LANES : (i + 1) * LANES]
@@ -368,39 +374,65 @@
     def emit(r, value):
         fin_b[r * LANES : (r + 1) * LANES, :] = value
 
-    run_chemistry(groups, species, LIT_CAP - FIRST, CHUNK_SECOND, mix, tab, state, made, emit)
+    def scatter_first(step):
+        at = pl.multiple_of(step * 2 * LANES, 2 * LANES)
+        got = jnp.dot(fin[...], pick[:FIRST, pl.ds(at, 2 * LANES)], preferred_element_type=f32)
+        for i in range(2):
+            back[pl.ds(2 * step + 1 + i, width, stride=8), :] = got[:, i * LANES : (i + 1) * LANES]
+
+    run_chemistry(
+        groups,
+        species,
+        LIT_CAP - FIRST,
+        CHUNK_SECOND,
+        mix,
+        tab,
+        state,
+        made,
+        emit,
+        scatter_first,
+    )
 
     def settle(j, got, moved):
         keep = lit_mask[j : j + 1, :]
         back[pl.ds(j, width, stride=8), :] = jnp.where(keep, got, moved.astype(f32))
 
-    for j in range(1, 7, 2):
-        cols = slice(j * LANES, (j + 2) * LANES)
-        got = jnp.dot(fin[...], pick[:FIRST, cols], preferred_element_type=f32)
-        got = got + jnp.dot(fin_b[...], pick[rest, cols], preferred_element_type=f32)
-        settle(j, got[:, :LANES], xb[:, j * LANES : (j + 1) * LANES])
-        settle(j + 1, got[:, LANES:], xb[:, (j + 1) * LANES : (j + 2) * LANES])
-    for i, j in enumerate((0, 7)):
-        got = jnp.dot(
-            fin_b[...], pick[rest, j * LANES : (j + 1) * LANES], preferred_element_type=f32
-        )
-        settle(j, got, xe[:, i * LANES : (i + 1) * LANES])
-
-    def finish(k, base):
-        for s in range(species):
-            at = pl.multiple_of((base + s) * 8, 8)
-            out[s * levels + k] = back[pl.ds(at, 8), :].astype(bf16)
+    for i in range(0, 8, 2):
+        cols = slice(i * LANES, (i + 2) * LANES)
+        got = jnp.dot(fin_b[...], pick[rest, cols], preferred_element_type=f32)
+        for h in range(2):
+            half = got[:, h * LANES : (h + 1) * LANES]
+            j = BLOCKS[i + h]
+            if i < 6:
+                half = half + back[pl.ds(j, width, stride=8), :]
+                settle(j, half, xb[:, (i + h) * LANES : (i + h + 1) * LANES])
+            else:
+                settle(j, half, xe[:, h * LANES : (h + 1) * LANES])
 
     whole_slots = levels // groups
-
-    def finish_body(j, carry):
-        for r in range(groups):
-            finish(j * groups + r, r * LANES + j * species)
-        return carry
-
-    lax.fori_loop(0, whole_slots, finish_body, 0)
-    for r in range(levels - whole_slots * groups):
-        finish(whole_slots * groups + r, r * LANES + whole_slots * species)
+    parts = 4
+    each = species // parts
+    copies = []
+    for part_at in range(parts):
+
+        def finish(k, base):
+            for s in range(part_at * each, (part_at + 1) * each):
+                at = pl.multiple_of((base + s) * 8, 8)
+                done[s * levels + k] = back[pl.ds(at, 8), :].astype(bf16)
+
+        def finish_body(j, carry):
+            for r in range(groups):
+                finish(j * groups + r, r * LANES + j * species)
+            return carry
+
+        lax.fori_loop(0, whole_slots, finish_body, 0)
+        for r in range(levels - whole_slots * groups):
+            finish(whole_slots * groups + r, r * LANES + whole_slots * species)
+        span = pl.ds(part_at * each * levels, each * levels)
+        copies.append(pltpu.make_async_copy(done.at[span], out.at[span], sent.at[part_at]))
+        copies[-1].start()
+    for copy in copies:
+        copy.wait()
 
 
 def local(tracers, east_wind, north_wind, sunlit, coupling, rate_table, rate_index, kappa):
@@ -441,20 +473,17 @@
     lat_a = lax.ppermute(send_a, "lat", pairs)
     lat_b = lax.ppermute(send_b, "lat", others) if others else jnp.zeros_like(send_b)
 
-    small = jnp.concatenate(
-        [jnp.pad(coupling, ((0, 0), (0, levels - species))), rate_table, jnp.pad(kappa, (0, 1))[None]]
-    )
     part, xb, pick, fin, mix, tab = pl.pallas_call(
         functools.partial(first_kernel, *sizes),
         out_shape=(
             shape((2, width, LANES), f32),
-            shape((width, 8 * LANES), bf16),
+            shape((width, 6 * LANES), bf16),
             shape((LIT_CAP, 8 * LANES), bf16),
             shape((width, FIRST), bf16),
             shape((groups, 2 * LANES, 2 * LANES), bf16),
             shape((16, LANES), f32),
         ),
-        in_specs=[smem] + [vmem] * 7,
+        in_specs=[smem] + [vmem] * 9,
         out_specs=(vmem,) * 6,
         scratch_shapes=[
             pltpu.VMEM((species + 1, 8, LANES), f32),
@@ -476,7 +505,9 @@
         sunlit,
         lon_a,
         lon_b,
-        small,
+        coupling,
+        rate_table,
+        kappa.reshape(1, levels - 1),
     )
 
     count = LIT_CAP - FIRST
@@ -484,13 +515,15 @@
         functools.partial(second_kernel, *sizes),
         out_shape=shape((species * levels, lat_rows, lon_cols), bf16),
         in_specs=[vmem] * 11,
-        out_specs=vmem,
+        out_specs=pl.BlockSpec(memory_space=pltpu.HBM),
         scratch_shapes=[
             pltpu.VMEM((width, 2 * LANES), bf16),
             pltpu.VMEM((width, count), bf16),
             pltpu.VMEM((groups, count, LANES), f32),
             pltpu.VMEM((groups, count, LANES), f32),
             pltpu.VMEM((width * 8, LANES), f32),
+            pltpu.VMEM((species * levels, lat_rows, LANES), bf16),
+            pltpu.SemaphoreType.DMA((4,)),
         ],
         compiler_params=pltpu.CompilerParams(vmem_limit_bytes=VMEM_LIMIT),
         name="second",

time: 48.8 us -> 48.3 us (0.990)
  Pallas kernels: 36.5 us -> 35.8 us
  other arithmetic: 0.7 us -> 0 us
  local copies, waits for them, and re-layouts: 0.04 us -> 0.73 us
    concatenate x1 -> x0, other arithmetic: 0.7 us -> none  [local(): jnp.concatenate([jnp.pad(coupling, ((0, 0), (0, levels - species))), rate...]
    unnamed x18 -> x20, local copies, waits for them, and re-layouts: 0.04 us -> 0.73 us
  transfers between devices with their start and end apart: 4 -> 4, of which waited for: 0 -> 0; matrix products, arithmetic and copies ran while one was open for 1% -> 0% of each run, Pallas kernels for 43% -> 43%
where the time goes in v4:
time: 48.3 us; the launch traced here: 48.1 us
  Pallas kernels  35.8 us (74%)
  starting transfers between devices  11.2 us (23%)
  local copies, waits for them, and re-layouts  0.73 us (2%)
    pallas_call x1, Pallas kernels, local(): pl.pallas_call(functools.partial(first_kernel, *sizes), out_shape=(shape(...  20.4 us
    pallas_call x1, Pallas kernels, local(): pl.pallas_call(functools.partial(second_kernel, *sizes), out_shape=shape(...  12.2 us
    ppermute x1, starting transfers between devices, local(): lax.ppermute(send_b, 'lat', others)  7.26 us
    pallas_call x1, Pallas kernels, local(): pl.pallas_call(functools.partial(edge_kernel, *sizes), out_shape=(shape((...  3.16 us
    ppermute x1, starting transfers between devices, local(): lon_a = lax.ppermute(lon_pack, 'lon', pairs)  1.82 us
    ppermute x1, starting transfers between devices, local(): lon_b = lax.ppermute(lon_pack, 'lon', others)  1.77 us
  transfers between devices with their start and end apart: 4, of which 0 were waited for; matrix products, arithmetic and copies ran while one was open for 0% of the time, Pallas kernels for 43%

profile of v4, /device:TPU:113, one launch (start us, length us, event | category | flops | bytes accessed | tf_op | source)
XLA Modules:
  0.0 48.1 jit_solution(905152757743138626)
XLA Ops:
  0.0 0.0 copy-start.3
  0.0 0.0 copy-start.2
  0.0 0.0 copy-start
  0.0 0.0 copy-start.5
  0.0 0.0 copy-start.9
  0.0 0.0 copy-start.8
  0.0 0.0 copy-start.7
  0.0 3.2 %edges.1 = (bf16[13,8,128]{2,1,0:T(8,128)(2,1)}, bf16[960,128]{1,0:T(8,128)(2,1)}, bf16[960,128]{1,0:T(8,128)(2,1)}, bf16[896,128]{1,0:T(8,128)(2,1)}, bf16[64,128]{1,0:T(8,128)(2,1)}) custom-call(bf16[768,8,128]{2,1,0:T(8,128)(2,1)} %bitcast.3, bf16[64,8,128]{2,1,0:T(8,128)(2,1)} %east.3, bf16[64,8,128]{2,1,0:T(8,128)(2,1)} %north.3), custom_call_target="tpu_custom_call" | custom-call | tf_op jit(solution)/shard_map/edges/pallas_call | solution.py:448
  3.2 1.8 %collective-permute-start.1 = (bf16[13,8,128]{2,1,0:T(8,128)(2,1)}, bf16[13,8,128]{2,1,0:T(8,128)(2,1)S(1)}, u32[]{:S(2)}, u32[]{:S(2)}) collective-permute-start(bf16[13,8,128]{2,1,0:T(8,128)(2,1)} %get-tuple-element.16), channel_id=1, source_target_pairs={{0,240},{16,32},{32,16},{48,64},{64,48},{80,96},{96,80},{112,128},... | collective-permute-start | bytes 79880 | tf_op jit(solution)/shard_map/ppermute | solution.py:470
  5.0 1.8 %collective-permute-start = (bf16[13,8,128]{2,1,0:T(8,128)(2,1)}, bf16[13,8,128]{2,1,0:T(8,128)(2,1)S(1)}, u32[]{:S(2)}, u32[]{:S(2)}) collective-permute-start(bf16[13,8,128]{2,1,0:T(8,128)(2,1)} %get-tuple-element.16), channel_id=1, source_target_pairs={{0,16},{16,0},{32,48},{48,32},{64,80},{80,64},{96,112},{112,96},{1... | collective-permute-start | bytes 79880 | tf_op jit(solution)/shard_map/ppermute | solution.py:469
  6.8 0.3 collective-permute-start.2
  7.2 7.3 %collective-permute-start.3 = (bf16[960,128]{1,0:T(8,128)(2,1)}, bf16[960,128]{1,0:T(8,128)(2,1)S(1)}, u32[]{:S(2)}, u32[]{:S(2)}) collective-permute-start(bf16[960,128]{1,0:T(8,128)(2,1)} %get-tuple-element.21), channel_id=1, source_target_pairs={{1,2},{2,1},{3,4},{4,3},{5,6},{6,5},{7,8},{8,7},{9,10},{10,9},{11,... | collective-permute-start | bytes 737288 | tf_op jit(solution)/shard_map/ppermute | solution.py:474
  14.4 0.0 collective-permute-done.1.lon_b
  14.4 0.0 collective-permute-done.lon_a
  14.4 0.0 copy-done.3
  14.5 0.0 copy-done.2
  14.5 0.0 copy-done
  14.5 0.0 copy-done.5
  14.5 0.0 copy-done.9
  14.5 0.0 copy-done.8
  14.5 0.0 copy-done.7
  14.5 0.0 copy-start.6
  14.5 0.7 %copy-done.6 = f32[12,12]{1,0:T(8,128)S(1)} copy-done((f32[12,12]{1,0:T(8,128)S(1)}, f32[12,12]{1,0:T(8,128)}, u32[]{:S(2)}) %copy-start.6) | copy-done | bytes 600
  15.2 0.0 copy-start.1
  15.2 0.0 copy-start.4
  15.2 20.4 %first.1 = (f32[2,896,128]{2,1,0:T(8,128)S(1)}, bf16[896,768]{1,0:T(8,128)(2,1)S(1)}, bf16[768,1024]{1,0:T(8,128)(2,1)S(1)}, bf16[896,512]{1,0:T(8,128)(2,1)S(1)...) custom-call(s32[12]{0:T(128)S(1)} %copy-done.8, bf16[768,8,128]{2,1,0:T(8,128)(2,1)S(1)} %bitcast.4, ...), custom_call_target="tpu_custom_call" | custom-call | flops 20000000000 | bytes 8000000 | tf_op jit(solution)/shard_map/first/pallas_call | solution.py:476
  35.7 0.0 collective-permute-done.2.lat_a
  35.7 0.0 collective-permute-done.3.lat_b
  35.7 0.0 copy-done.1
  35.7 0.0 copy-done.4
  35.7 12.2 %second.1 = bf16[768,8,128]{2,1,0:T(8,128)(2,1)} custom-call(f32[2,896,128]{2,1,0:T(8,128)S(1)} %get-tuple-element.17.part, bf16[896,128]{1,0:T(8,128)(2,1)S(1)} %copy-done.1, bf16[64,128]{1,0:T(8,128)(2,1)S(1)} %copy-done.4, bf16[960,128]{1,0:T(8,128)(2,1)S(1)} %collective-permute-done.2.lat_a, bf16[960,128]{1,0:T(8,128)(2,1)S(1)} %collective-permute-done.3.lat_b, ...), custom_call_target="tpu_custom_call" | custom-call | tf_op jit(solution)/shard_map/second/pallas_call | solution.py:514
Async XLA Ops:
  0.0 14.4 %copy-start.3 = (bf16[64,8,128]{2,1,0:T(8,128)(2,1)S(1)}, bf16[64,8,128]{2,1,0:T(8,128)(2,1)}, u32[]{:S(2)}) copy-start(bf16[64,8,128]{2,1,0:T(8,128)(2,1)} %north.3) | copy-start | bytes 393220
  0.0 14.5 %copy-start.2 = (bf16[64,8,128]{2,1,0:T(8,128)(2,1)S(1)}, bf16[64,8,128]{2,1,0:T(8,128)(2,1)}, u32[]{:S(2)}) copy-start(bf16[64,8,128]{2,1,0:T(8,128)(2,1)} %east.3) | copy-start | bytes 393220
  0.0 14.5 %copy-start = (bf16[12,64,8,128]{3,2,1,0:T(8,128)(2,1)S(1)}, bf16[12,64,8,128]{3,2,1,0:T(8,128)(2,1)}, u32[]{:S(2)}) copy-start(bf16[12,64,8,128]{3,2,1,0:T(8,128)(2,1)} %param.8) | copy-start | bytes 4718596
  0.0 14.5 %copy-start.5 = (s32[8,128]{1,0:T(8,128)S(1)}, s32[8,128]{1,0:T(8,128)}, u32[]{:S(2)}) copy-start(s32[8,128]{1,0:T(8,128)} %lit.3) | copy-start | bytes 12292
  0.0 14.5 %copy-start.9 = (f32[63]{0:T(128)S(1)}, f32[63]{0:T(128)}, u32[]{:S(2)}) copy-start(f32[63]{0:T(128)} %param.15) | copy-start | bytes 760
  0.0 14.5 %copy-start.8 = (s32[12]{0:T(128)S(1)}, s32[12]{0:T(128)}, u32[]{:S(2)}) copy-start(s32[12]{0:T(128)} %rate_index.1) | copy-start | bytes 148
  0.0 14.5 %copy-start.7 = (f32[8,64]{1,0:T(8,128)S(1)}, f32[8,64]{1,0:T(8,128)}, u32[]{:S(2)}) copy-start(f32[8,64]{1,0:T(8,128)} %rate_table.1) | copy-start | bytes 6148
  3.2 11.2 %collective-permute-start.1 = (bf16[13,8,128]{2,1,0:T(8,128)(2,1)}, bf16[13,8,128]{2,1,0:T(8,128)(2,1)S(1)}, u32[]{:S(2)}, u32[]{:S(2)}) collective-permute-start(bf16[13,8,128]{2,1,0:T(8,128)(2,1)} %get-tuple-element.16), channel_id=1, source_target_pairs={{0,240},{16,32},{32,16},{48,64},{64,48},{80,96},{96,80},{112,128},... | collective-permute-start | bytes 79880 | tf_op jit(solution)/shard_map/ppermute | solution.py:470
  5.0 9.5 %collective-permute-start = (bf16[13,8,128]{2,1,0:T(8,128)(2,1)}, bf16[13,8,128]{2,1,0:T(8,128)(2,1)S(1)}, u32[]{:S(2)}, u32[]{:S(2)}) collective-permute-start(bf16[13,8,128]{2,1,0:T(8,128)(2,1)} %get-tuple-element.16), channel_id=1, source_target_pairs={{0,16},{16,0},{32,48},{48,32},{64,80},{80,64},{96,112},{112,96},{1... | collective-permute-start | bytes 79880 | tf_op jit(solution)/shard_map/ppermute | solution.py:469
  6.8 28.9 %collective-permute-start.2 = (bf16[960,128]{1,0:T(8,128)(2,1)}, bf16[960,128]{1,0:T(8,128)(2,1)S(1)}, u32[]{:S(2)}, u32[]{:S(2)}) collective-permute-start(bf16[960,128]{1,0:T(8,128)(2,1)} %get-tuple-element.20), channel_id=1, source_target_pairs={{0,1},{1,0},{2,3},{3,2},{4,5},{5,4},{6,7},{7,6},{8,9},{9,8},{10,11... | collective-permute-start | bytes 737288 | tf_op jit(solution)/shard_map/ppermute | solution.py:473
  7.2 28.5 %collective-permute-start.3 = (bf16[960,128]{1,0:T(8,128)(2,1)}, bf16[960,128]{1,0:T(8,128)(2,1)S(1)}, u32[]{:S(2)}, u32[]{:S(2)}) collective-permute-start(bf16[960,128]{1,0:T(8,128)(2,1)} %get-tuple-element.21), channel_id=1, source_target_pairs={{1,2},{2,1},{3,4},{4,3},{5,6},{6,5},{7,8},{8,7},{9,10},{10,9},{11,... | collective-permute-start | bytes 737288 | tf_op jit(solution)/shard_map/ppermute | solution.py:474
  14.5 0.7 %copy-start.6 = (f32[12,12]{1,0:T(8,128)S(1)}, f32[12,12]{1,0:T(8,128)}, u32[]{:S(2)}) copy-start(f32[12,12]{1,0:T(8,128)} %coupling.1) | copy-start | bytes 1732
  15.2 20.5 %copy-start.1 = (bf16[896,128]{1,0:T(8,128)(2,1)S(1)}, bf16[896,128]{1,0:T(8,128)(2,1)}, u32[]{:S(2)}) copy-start(bf16[896,128]{1,0:T(8,128)(2,1)} %get-tuple-element.18.top) | copy-start | bytes 688132
  15.2 20.5 %copy-start.4 = (bf16[64,128]{1,0:T(8,128)(2,1)S(1)}, bf16[64,128]{1,0:T(8,128)(2,1)}, u32[]{:S(2)}) copy-start(bf16[64,128]{1,0:T(8,128)(2,1)} %get-tuple-element.19.wind) | copy-start | bytes 49156

commit v5 on v4

--- a/solution.py
+++ b/solution.py
@@ -228,9 +228,9 @@
         )
         v_next = jnp.where(sub == 7, 0.0, pltpu.roll(v, 7, 0))
         a_west = jnp.maximum(u, 0.0)
-        a_east = -jnp.minimum(u_next, 0.0)
+        a_east = jnp.minimum(u_next, 0.0)
         a_south = jnp.where(sub == 0, 0.0, jnp.maximum(v, 0.0))
-        a_north = -jnp.minimum(v_next, 0.0)
+        a_north = jnp.minimum(v_next, 0.0)
         a_here = (
             1.0
             - (jnp.maximum(u_next, 0.0) - jnp.minimum(u, 0.0))
@@ -244,9 +244,9 @@
             new = (
                 a_here * c
                 + a_west * west
-                + a_east * east_c
+                - a_east * east_c
                 + a_south * pltpu.roll(c, 1, 0)
-                + a_north * pltpu.roll(c, 7, 0)
+                - a_north * pltpu.roll(c, 7, 0)
             )
             at = pl.multiple_of((base + s) * 8, 8)
             adv[pl.ds(at, 8), :] = new

time: 48.3 us -> 48.3 us (level)
  transfers between devices with their start and end apart: 4 -> 4, of which waited for: 0 -> 0; matrix products, arithmetic and copies ran while one was open for 0% -> 0% of each run, Pallas kernels for 43% -> 42%
where the time goes in v5:
time: 48.3 us; the launch traced here: 48.1 us
  Pallas kernels  35.8 us (74%)
  starting transfers between devices  11.2 us (23%)
  local copies, waits for them, and re-layouts  0.73 us (2%)
    pallas_call x1, Pallas kernels, local(): pl.pallas_call(functools.partial(first_kernel, *sizes), out_shape=(shape(...  20.4 us
    pallas_call x1, Pallas kernels, local(): pl.pallas_call(functools.partial(second_kernel, *sizes), out_shape=shape(...  12.2 us
    ppermute x1, starting transfers between devices, local(): lax.ppermute(send_b, 'lat', others)  7.26 us
    pallas_call x1, Pallas kernels, local(): pl.pallas_call(functools.partial(edge_kernel, *sizes), out_shape=(shape((...  3.16 us
    ppermute x1, starting transfers between devices, local(): lon_a = lax.ppermute(lon_pack, 'lon', pairs)  1.82 us
    ppermute x1, starting transfers between devices, local(): lon_b = lax.ppermute(lon_pack, 'lon', others)  1.77 us
  transfers between devices with their start and end apart: 4, of which 0 were waited for; matrix products, arithmetic and copies ran while one was open for 0% of the time, Pallas kernels for 42%

profile of v5, /device:TPU:113, one launch (start us, length us, event | category | flops | bytes accessed | tf_op | source)
XLA Modules:
  0.0 48.1 jit_solution(10584785899127796162)
XLA Ops:
  0.0 0.0 copy-start.3
  0.0 0.0 copy-start.2
  0.0 0.0 copy-start
  0.0 0.0 copy-start.5
  0.0 0.0 copy-start.9
  0.0 0.0 copy-start.8
  0.0 0.0 copy-start.7
  0.0 3.2 %edges.1 = (bf16[13,8,128]{2,1,0:T(8,128)(2,1)}, bf16[960,128]{1,0:T(8,128)(2,1)}, bf16[960,128]{1,0:T(8,128)(2,1)}, bf16[896,128]{1,0:T(8,128)(2,1)}, bf16[64,128]{1,0:T(8,128)(2,1)}) custom-call(bf16[768,8,128]{2,1,0:T(8,128)(2,1)} %bitcast.3, bf16[64,8,128]{2,1,0:T(8,128)(2,1)} %east.3, bf16[64,8,128]{2,1,0:T(8,128)(2,1)} %north.3), custom_call_target="tpu_custom_call" | custom-call | tf_op jit(solution)/shard_map/edges/pallas_call | solution.py:448
  3.2 1.8 %collective-permute-start.1 = (bf16[13,8,128]{2,1,0:T(8,128)(2,1)}, bf16[13,8,128]{2,1,0:T(8,128)(2,1)S(1)}, u32[]{:S(2)}, u32[]{:S(2)}) collective-permute-start(bf16[13,8,128]{2,1,0:T(8,128)(2,1)} %get-tuple-element.16), channel_id=1, source_target_pairs={{0,240},{16,32},{32,16},{48,64},{64,48},{80,96},{96,80},{112,128},... | collective-permute-start | bytes 79880 | tf_op jit(solution)/shard_map/ppermute | solution.py:470
  5.0 1.8 %collective-permute-start = (bf16[13,8,128]{2,1,0:T(8,128)(2,1)}, bf16[13,8,128]{2,1,0:T(8,128)(2,1)S(1)}, u32[]{:S(2)}, u32[]{:S(2)}) collective-permute-start(bf16[13,8,128]{2,1,0:T(8,128)(2,1)} %get-tuple-element.16), channel_id=1, source_target_pairs={{0,16},{16,0},{32,48},{48,32},{64,80},{80,64},{96,112},{112,96},{1... | collective-permute-start | bytes 79880 | tf_op jit(solution)/shard_map/ppermute | solution.py:469
  6.8 0.3 collective-permute-start.2
  7.2 7.3 %collective-permute-start.3 = (bf16[960,128]{1,0:T(8,128)(2,1)}, bf16[960,128]{1,0:T(8,128)(2,1)S(1)}, u32[]{:S(2)}, u32[]{:S(2)}) collective-permute-start(bf16[960,128]{1,0:T(8,128)(2,1)} %get-tuple-element.21), channel_id=1, source_target_pairs={{1,2},{2,1},{3,4},{4,3},{5,6},{6,5},{7,8},{8,7},{9,10},{10,9},{11,... | collective-permute-start | bytes 737288 | tf_op jit(solution)/shard_map/ppermute | solution.py:474
  14.4 0.0 collective-permute-done.1.lon_b
  14.4 0.0 collective-permute-done.lon_a
  14.4 0.0 copy-done.3
  14.5 0.0 copy-done.2
  14.5 0.0 copy-done
  14.5 0.0 copy-done.5
  14.5 0.0 copy-done.9
  14.5 0.0 copy-done.8
  14.5 0.0 copy-done.7
  14.5 0.0 copy-start.6
  14.5 0.7 %copy-done.6 = f32[12,12]{1,0:T(8,128)S(1)} copy-done((f32[12,12]{1,0:T(8,128)S(1)}, f32[12,12]{1,0:T(8,128)}, u32[]{:S(2)}) %copy-start.6) | copy-done | bytes 600
  15.2 0.0 copy-start.1
  15.2 0.0 copy-start.4
  15.2 20.4 %first.1 = (f32[2,896,128]{2,1,0:T(8,128)S(1)}, bf16[896,768]{1,0:T(8,128)(2,1)S(1)}, bf16[768,1024]{1,0:T(8,128)(2,1)S(1)}, bf16[896,512]{1,0:T(8,128)(2,1)S(1)...) custom-call(s32[12]{0:T(128)S(1)} %copy-done.8, bf16[768,8,128]{2,1,0:T(8,128)(2,1)S(1)} %bitcast.4, ...), custom_call_target="tpu_custom_call" | custom-call | flops 20000000000 | bytes 8000000 | tf_op jit(solution)/shard_map/first/pallas_call | solution.py:476
  35.7 0.0 collective-permute-done.2.lat_a
  35.7 0.0 collective-permute-done.3.lat_b
  35.7 0.0 copy-done.1
  35.7 0.0 copy-done.4
  35.7 12.2 %second.1 = bf16[768,8,128]{2,1,0:T(8,128)(2,1)} custom-call(f32[2,896,128]{2,1,0:T(8,128)S(1)} %get-tuple-element.17.part, bf16[896,128]{1,0:T(8,128)(2,1)S(1)} %copy-done.1, bf16[64,128]{1,0:T(8,128)(2,1)S(1)} %copy-done.4, bf16[960,128]{1,0:T(8,128)(2,1)S(1)} %collective-permute-done.2.lat_a, bf16[960,128]{1,0:T(8,128)(2,1)S(1)} %collective-permute-done.3.lat_b, ...), custom_call_target="tpu_custom_call" | custom-call | tf_op jit(solution)/shard_map/second/pallas_call | solution.py:514
Async XLA Ops:
  0.0 14.4 %copy-start.3 = (bf16[64,8,128]{2,1,0:T(8,128)(2,1)S(1)}, bf16[64,8,128]{2,1,0:T(8,128)(2,1)}, u32[]{:S(2)}) copy-start(bf16[64,8,128]{2,1,0:T(8,128)(2,1)} %north.3) | copy-start | bytes 393220
  0.0 14.5 %copy-start.2 = (bf16[64,8,128]{2,1,0:T(8,128)(2,1)S(1)}, bf16[64,8,128]{2,1,0:T(8,128)(2,1)}, u32[]{:S(2)}) copy-start(bf16[64,8,128]{2,1,0:T(8,128)(2,1)} %east.3) | copy-start | bytes 393220
  0.0 14.5 %copy-start = (bf16[12,64,8,128]{3,2,1,0:T(8,128)(2,1)S(1)}, bf16[12,64,8,128]{3,2,1,0:T(8,128)(2,1)}, u32[]{:S(2)}) copy-start(bf16[12,64,8,128]{3,2,1,0:T(8,128)(2,1)} %param.8) | copy-start | bytes 4718596
  0.0 14.5 %copy-start.5 = (s32[8,128]{1,0:T(8,128)S(1)}, s32[8,128]{1,0:T(8,128)}, u32[]{:S(2)}) copy-start(s32[8,128]{1,0:T(8,128)} %lit.3) | copy-start | bytes 12292
  0.0 14.5 %copy-start.9 = (f32[63]{0:T(128)S(1)}, f32[63]{0:T(128)}, u32[]{:S(2)}) copy-start(f32[63]{0:T(128)} %param.15) | copy-start | bytes 760
  0.0 14.5 %copy-start.8 = (s32[12]{0:T(128)S(1)}, s32[12]{0:T(128)}, u32[]{:S(2)}) copy-start(s32[12]{0:T(128)} %rate_index.1) | copy-start | bytes 148
  0.0 14.5 %copy-start.7 = (f32[8,64]{1,0:T(8,128)S(1)}, f32[8,64]{1,0:T(8,128)}, u32[]{:S(2)}) copy-start(f32[8,64]{1,0:T(8,128)} %rate_table.1) | copy-start | bytes 6148
  3.2 11.2 %collective-permute-start.1 = (bf16[13,8,128]{2,1,0:T(8,128)(2,1)}, bf16[13,8,128]{2,1,0:T(8,128)(2,1)S(1)}, u32[]{:S(2)}, u32[]{:S(2)}) collective-permute-start(bf16[13,8,128]{2,1,0:T(8,128)(2,1)} %get-tuple-element.16), channel_id=1, source_target_pairs={{0,240},{16,32},{32,16},{48,64},{64,48},{80,96},{96,80},{112,128},... | collective-permute-start | bytes 79880 | tf_op jit(solution)/shard_map/ppermute | solution.py:470
  5.0 9.5 %collective-permute-start = (bf16[13,8,128]{2,1,0:T(8,128)(2,1)}, bf16[13,8,128]{2,1,0:T(8,128)(2,1)S(1)}, u32[]{:S(2)}, u32[]{:S(2)}) collective-permute-start(bf16[13,8,128]{2,1,0:T(8,128)(2,1)} %get-tuple-element.16), channel_id=1, source_target_pairs={{0,16},{16,0},{32,48},{48,32},{64,80},{80,64},{96,112},{112,96},{1... | collective-permute-start | bytes 79880 | tf_op jit(solution)/shard_map/ppermute | solution.py:469
  6.8 28.9 %collective-permute-start.2 = (bf16[960,128]{1,0:T(8,128)(2,1)}, bf16[960,128]{1,0:T(8,128)(2,1)S(1)}, u32[]{:S(2)}, u32[]{:S(2)}) collective-permute-start(bf16[960,128]{1,0:T(8,128)(2,1)} %get-tuple-element.20), channel_id=1, source_target_pairs={{0,1},{1,0},{2,3},{3,2},{4,5},{5,4},{6,7},{7,6},{8,9},{9,8},{10,11... | collective-permute-start | bytes 737288 | tf_op jit(solution)/shard_map/ppermute | solution.py:473
  7.2 28.5 %collective-permute-start.3 = (bf16[960,128]{1,0:T(8,128)(2,1)}, bf16[960,128]{1,0:T(8,128)(2,1)S(1)}, u32[]{:S(2)}, u32[]{:S(2)}) collective-permute-start(bf16[960,128]{1,0:T(8,128)(2,1)} %get-tuple-element.21), channel_id=1, source_target_pairs={{1,2},{2,1},{3,4},{4,3},{5,6},{6,5},{7,8},{8,7},{9,10},{10,9},{11,... | collective-permute-start | bytes 737288 | tf_op jit(solution)/shard_map/ppermute | solution.py:474
  14.5 0.7 %copy-start.6 = (f32[12,12]{1,0:T(8,128)S(1)}, f32[12,12]{1,0:T(8,128)}, u32[]{:S(2)}) copy-start(f32[12,12]{1,0:T(8,128)} %coupling.1) | copy-start | bytes 1732
  15.2 20.5 %copy-start.1 = (bf16[896,128]{1,0:T(8,128)(2,1)S(1)}, bf16[896,128]{1,0:T(8,128)(2,1)}, u32[]{:S(2)}) copy-start(bf16[896,128]{1,0:T(8,128)(2,1)} %get-tuple-element.18.top) | copy-start | bytes 688132
  15.2 20.5 %copy-start.4 = (bf16[64,128]{1,0:T(8,128)(2,1)S(1)}, bf16[64,128]{1,0:T(8,128)(2,1)}, u32[]{:S(2)}) copy-start(bf16[64,128]{1,0:T(8,128)(2,1)} %get-tuple-element.19.wind) | copy-start | bytes 49156
